TPU v7x, 256 devices: a whole 4x4x8 slice. The times are simulated.
256 devices in a mesh: wide: 64 (over z, y, core), narrow: 4 (over x).
Axes of the slice: x: 4, y: 4, z: 8, core: 2. Of those that a mesh axis runs over, the one named last changes fastest.
Arguments:
- hidden_in: bfloat16 [1024, 4096], P('narrow', 'wide'), may hold values from -0.59765625 to 0.59765625
- cached_len: int32 [4], replicated, may hold values from 1 to 4096, 8192 in all
- k_cache: bfloat16 [4, 32768, 128], P('narrow', 'wide'), may hold values from -256 to 256
- v_cache: bfloat16 [4, 32768, 128], P('narrow', 'wide'), may hold values from -24 to 24
- attn_gain: bfloat16 [4096], replicated, may hold values from 0.099609375 to 1.8984375
- ffn_gain: bfloat16 [4096], replicated, may hold values from 0.099609375 to 1.8984375
- wqkv: bfloat16 [6144, 4096], P('wide', 'narrow'), may hold values from -0.09375 to 0.09375
- wo: bfloat16 [4096, 4096], P('wide', 'narrow'), may hold values from -0.09375 to 0.09375
- wgate: bfloat16 [14336, 4096], P('wide', 'narrow'), may hold values from -0.09375 to 0.09375
- wup: bfloat16 [14336, 4096], P('wide', 'narrow'), may hold values from -0.09375 to 0.09375
- wdown: bfloat16 [14336, 4096], P('wide', 'narrow'), may hold values from -0.125 to 0.125
Outputs:
- hidden_out: bfloat16 [1024, 4096], P('narrow', 'wide')
- new_k_cache: bfloat16 [4, 32768, 128], P('narrow', 'wide')
- new_v_cache: bfloat16 [4, 32768, 128], P('narrow', 'wide')
All inputs are finite; a program needn't handle non-finite values.
Results may differ from a plain program's by a relative error of at most 0.018.
The roundings to bfloat16 on the way count: a program that leaves them out, or rounds other values in their place, can miss the bound.
Values may be sent and summed in bfloat16 or wider, within the bound.
A program may use at most 64 MiB of HBM per device.

v0:
```python
import jax
import jax.numpy as jnp
from jax import lax
from jax.sharding import PartitionSpec as P

QH = 32
KVH = 8
HD = 128
WINDOW = 4096


NEG_FILL = -1e30


def partner(block, axis, stride):
    count = lax.axis_size(axis)
    route = []
    for low in range(count):
        high = low | 1 << stride
        if high != low and high < count:
            route += [(low, high), (high, low)]
    return lax.ppermute(block, axis, route)


def rms_scale(values, weights):
    widened = values.astype(jnp.float32)
    mean_square = jnp.mean(widened * widened, axis=-1, keepdims=True)
    return (widened * lax.rsqrt(mean_square + 1e-05) * weights.astype(jnp.float32)).astype(
        jnp.bfloat16
    )


def times_rows(left, right):
    return lax.dot_general(
        left, right, (((1,), (1,)), ((), ())), preferred_element_type=jnp.float32
    )


def rotate(heads, positions):
    half_width = heads.shape[-1] // 2
    exponent = jnp.arange(half_width, dtype=jnp.float32) * (2.0 / heads.shape[-1])
    frequency = jnp.power(10000.0, -exponent)
    angles = positions.astype(jnp.float32)[:, None] * frequency[None, :]
    cosine = jnp.cos(angles)[:, None, :]
    sine = jnp.sin(angles)[:, None, :]
    widened = heads.astype(jnp.float32)
    first_half = widened[..., :half_width]
    second_half = widened[..., half_width:]
    return jnp.concatenate(
        [first_half * cosine - second_half * sine, second_half * cosine + first_half * sine],
        axis=-1,
    ).astype(jnp.bfloat16)


def gather_cols(block):
    return lax.all_gather(block, "wide", axis=1, tiled=True)


def collect_heads(qkv_piece, sections):
    position = lax.axis_index("wide")
    for bit_index in range(sections):
        other_piece = partner(qkv_piece, "wide", bit_index)
        upper_half = position // 2**bit_index % 2 == 1
        qkv_piece = jnp.where(
            upper_half,
            jnp.concatenate([other_piece, qkv_piece], axis=1),
            jnp.concatenate([qkv_piece, other_piece], axis=1),
        )
    return qkv_piece


def combine(earlier, later):
    highest = jnp.maximum(earlier[0], later[0])
    left_scale = jnp.exp(earlier[0] - highest)
    right_scale = jnp.exp(later[0] - highest)
    return (
        highest,
        earlier[1] * left_scale + later[1] * right_scale,
        earlier[2] * left_scale[..., None] + later[2] * right_scale[..., None],
    )


def empty_state(row_count, group_size):
    return (
        jnp.full((row_count, group_size), NEG_FILL, jnp.float32),
        jnp.zeros((row_count, group_size), jnp.float32),
        jnp.zeros((row_count, group_size, HD), jnp.float32),
    )


def attend(queries, query_pos, keys, values, key_pos, key_live, soft_state):
    row_count, group_size, head_width = queries.shape
    flat_queries = queries.reshape(row_count * group_size, head_width)
    key_count = keys.shape[0]
    block_size = min(512, key_count)
    block_count = key_count // block_size
    lowest = jnp.min(query_pos)
    highest = jnp.max(query_pos)

    def key_step(carry, blocks):
        key_block, value_block, pos_block, live_block = blocks

        def score_block(running):
            peak_old, totals, accum = running
            scores = jnp.einsum(
                "qd,kd->qk", flat_queries, key_block, preferred_element_type=jnp.float32
            )
            scores = scores.reshape(row_count, group_size, block_size) * HD ** (-0.5)
            allowed = (
                live_block[None, :]
                & (pos_block[None, :] <= query_pos[:, None])
                & (pos_block[None, :] > query_pos[:, None] - WINDOW)
            )
            allowed = allowed[:, None, :]
            scores = jnp.where(allowed, scores, NEG_FILL)
            peak_new = jnp.maximum(peak_old, jnp.max(scores, axis=-1))
            factor = jnp.exp(peak_old - peak_new)
            exp_terms = jnp.where(allowed, jnp.exp(scores - peak_new[..., None]), 0.0)
            totals = totals * factor + jnp.sum(exp_terms, axis=-1)
            weights = exp_terms.astype(jnp.bfloat16).reshape(row_count * group_size, block_size)
            mixed = jnp.dot(weights, value_block, preferred_element_type=jnp.float32).reshape(
                row_count, group_size, head_width
            )
            return (peak_new, totals, accum * factor[..., None] + mixed)

        useful = jnp.any(live_block & (pos_block <= highest) & (pos_block > lowest - WINDOW))
        return (lax.cond(useful, score_block, lambda unchanged: unchanged, carry), None)

    blocks = (
        keys.reshape(block_count, block_size, head_width),
        values.reshape(block_count, block_size, head_width),
        key_pos.reshape(block_count, block_size),
        key_live.reshape(block_count, block_size),
    )
    soft_state, _ = lax.scan(key_step, soft_state, blocks)
    return soft_state


def per_device(
    hidden_in, cached_len, k_cache, v_cache, attn_gain, ffn_gain, wqkv, wo, wgate, wup, wdown
):
    qkv_full, out_full, gate_full, up_full, down_full = (
        lax.all_gather(wqkv, "narrow", axis=1, tiled=True),
        lax.all_gather(wo, "narrow", axis=1, tiled=True),
        lax.all_gather(wgate, "narrow", axis=1, tiled=True),
        lax.all_gather(wup, "narrow", axis=1, tiled=True),
        lax.all_gather(wdown, "narrow", axis=1, tiled=True),
    )
    wide_count = lax.axis_size("wide")
    part_count = wide_count // KVH
    sections = part_count.bit_length() - 1
    position = lax.axis_index("wide")
    part_index = position % part_count
    length = cached_len[lax.axis_index("narrow")]
    span_len = hidden_in.shape[0]
    group_size = QH // KVH
    steps_t = jnp.arange(span_len, dtype=jnp.int32)
    query_pos = length + steps_t
    normed_attn = rms_scale(gather_cols(hidden_in), attn_gain)
    qkv_piece = times_rows(normed_attn, qkv_full).astype(jnp.bfloat16)
    grouped = collect_heads(qkv_piece, sections)
    queries = rotate(grouped[:, : group_size * HD].reshape(span_len, group_size, HD), query_pos)
    new_keys = rotate(
        grouped[:, group_size * HD : (group_size + 1) * HD].reshape(span_len, 1, HD), query_pos
    ).reshape(span_len, HD)
    new_vals = grouped[:, (group_size + 1) * HD :]
    cache_keys = k_cache[0]
    cache_vals = v_cache[0]
    block_slots = cache_keys.shape[0]
    slot_pos = part_index * block_slots + jnp.arange(block_slots, dtype=jnp.int32)
    share_rows = span_len // part_count
    start_row = part_index * share_rows
    soft_state = empty_state(span_len, group_size)
    soft_state = attend(
        queries, query_pos, cache_keys, cache_vals, slot_pos, slot_pos < length, soft_state
    )
    soft_state = attend(
        queries,
        query_pos,
        lax.dynamic_slice_in_dim(new_keys, start_row, share_rows, 0),
        lax.dynamic_slice_in_dim(new_vals, start_row, share_rows, 0),
        lax.dynamic_slice_in_dim(query_pos, start_row, share_rows, 0),
        jnp.ones((share_rows,), jnp.bool_),
        soft_state,
    )
    for bit_index in range(sections):
        soft_state = combine(soft_state, partner(soft_state, "wide", bit_index))
    attended = (
        (soft_state[2] / soft_state[1][..., None])
        .astype(jnp.bfloat16)
        .reshape(span_len, group_size * HD)
    )
    width_share = group_size * HD // part_count
    own_cols = lax.dynamic_slice_in_dim(attended, part_index * width_share, width_share, 1)
    mixed_heads = gather_cols(own_cols)
    projected = times_rows(mixed_heads, out_full)
    after_attn = (hidden_in.astype(jnp.float32) + projected).astype(jnp.bfloat16)
    whole_after = gather_cols(after_attn)
    normed_ffn = rms_scale(whole_after, ffn_gain)
    gate_proj = times_rows(normed_ffn, gate_full)
    up_proj = times_rows(normed_ffn, up_full)
    activation = (jax.nn.silu(gate_proj) * up_proj).astype(jnp.bfloat16)
    summed = lax.psum_scatter(
        lax.dot_general(
            down_full, activation, (((0,), (1,)), ((), ())), preferred_element_type=jnp.float32
        ),
        "wide",
        scatter_dimension=0,
        tiled=True,
    )
    hidden_out = (after_attn.astype(jnp.float32) + summed.T).astype(jnp.bfloat16)
    offset = (slot_pos - length) % WINDOW
    fresh_slot = offset < span_len
    pick_row = jnp.minimum(offset, span_len - 1)
    new_k_cache = jnp.where(fresh_slot[:, None], jnp.take(new_keys, pick_row, axis=0), cache_keys)[
        None
    ]
    new_v_cache = jnp.where(fresh_slot[:, None], jnp.take(new_vals, pick_row, axis=0), cache_vals)[
        None
    ]
    return (hidden_out, new_k_cache, new_v_cache)


def solution(mesh):
    return jax.shard_map(
        per_device,
        mesh=mesh,
        in_specs=(
            P("narrow", "wide"),
            P(),
            P("narrow", "wide", None),
            P("narrow", "wide", None),
            P(),
            P(),
            P("wide", "narrow"),
            P("wide", "narrow"),
            P("wide", "narrow"),
            P("wide", "narrow"),
            P("wide", "narrow"),
        ),
        out_specs=(P("narrow", "wide"), P("narrow", "wide", None), P("narrow", "wide", None)),
        check_vma=False,
    )
```

profile of v0, /device:TPU:1, one launch (start us, length us, event | category | flops | bytes accessed | tf_op | source)
XLA Modules:
  0.0 565.6 jit_solution(13301387686112721194)
XLA Ops:
  8.0 1.3 dynamic_slice.37
  9.2 1.2 fusion.63
  10.5 1.2 fusion.64
  13.1 2.0 fusion.58
  15.7 13.1 %all_gather.25 = bf16[96,4096]{1,0:T(8,128)(2,1)S(1)} all-gather(bf16[96,1024]{1,0:T(8,128)(2,1)} %param.23), channel_id=1, replica_groups=mesh['wide'=64,'narrow'=4] {'narrow'}, dimensions={1}, use_global_device_ids=true | all-gather | bytes 983040 | tf_op jit(solution)/shard_map/all_gather | solution.py:143
  28.8 63.5 %all-gather.7.cloned.1.call-done = bf16[256,4096]{0,1:T(8,128)(2,1)} async-done(((bf16[256,64]{0,1:T(8,128)(2,1)}), bf16[256,4096]{0,1:T(8,128)(2,1)}) %all-gather.7.cloned.1.call-update) | async-done | bytes 2097168 | tf_op jit(solution)/shard_map/all_gather | solution.py:56
  92.3 2.3 fusion.16
  94.7 0.8 fusion.27
  95.8 1.9 and_reduce_fusion
  100.1 3.9 collective-permute-done.1
  104.1 1.9 collective-permute-start.2
  106.3 4.7 collective-permute-done.2
  113.4 11.8 %conditional.2 = ((f32[256,4]{1,0:T(8,128)S(1)}, f32[256,4]{1,0:T(8,128)}, f32[256,4,128]{2,0,1:T(8,128)S(1)})) conditional(s32[]{:T(128)} %convert_element_type.91, (f32[256,4]{1,0:T(8,128)S(1)}, f32[256,4]{1,0:T(8,128)}, f32[256,4,128]{2,0,1:T(8,128)S(1)}) %tuple.31, (pred[512]{0:T(512)(128)(4,1)S(1)}, s32[512]{0:T(512)S(1)}, s32[256]{0:T(256)S(1)}, ...), branch_computations={%region_5.6_spmd, %region_6.9_spmd} | conditional | flops 273942784 | bytes 13486680 | solution.py:127
  114.7 1.5 fusion
  116.1 0.8 reduce_max.28
  116.9 1.6 max.12
  118.5 1.0 sub.66
  119.5 1.8 fusion.1
  121.5 1.7 multiply_add_fusion
  123.2 1.4 dot_general.9
  125.2 4.8 conditional.3
  125.3 0.7 compare_and_fusion.1
  126.5 0.9 copy.56
  128.1 0.9 multiply_add_fusion.1
  130.0 2.1 collective-permute-start.4
  132.6 1.0 collective-permute-done.3
  134.1 1.2 collective-permute-start.10
  135.6 11.5 %collective-permute-done.10 = f32[256,4]{0,1:T(4,128)S(1)} collective-permute-done((f32[256,4]{0,1:T(4,128)S(1)}, f32[256,4]{0,1:T(4,128)S(1)}, u32[]{:S(2)}, u32[]{:S(2)}) %collective-permute-start.10) | collective-permute-done | bytes 4128 | tf_op jit(solution)/shard_map/ppermute | solution.py:22
  147.3 1.9 collective-permute-start.8
  149.2 1.1 collective-permute-start.11
  150.3 1.8 collective-permute-start.7
  152.2 9.0 %collective-permute-done.11 = f32[256,4]{0,1:T(4,128)S(1)} collective-permute-done((f32[256,4]{0,1:T(4,128)S(1)}, f32[256,4]{0,1:T(4,128)S(1)}, u32[]{:S(2)}, u32[]{:S(2)}) %collective-permute-start.11) | collective-permute-done | bytes 4128 | tf_op jit(solution)/shard_map/ppermute | solution.py:22
  162.1 10.2 %all_gather.27 = bf16[64,4096]{1,0:T(8,128)(2,1)S(1)} all-gather(bf16[64,1024]{1,0:T(8,128)(2,1)S(1)} %copy-done.14), channel_id=1, replica_groups=mesh['wide'=64,'narrow'=4] {'narrow'}, dimensions={1}, use_global_device_ids=true | all-gather | bytes 655360 | tf_op jit(solution)/shard_map/all_gather | solution.py:144
  172.3 65.4 %all-gather.9.cloned.1.call-done = bf16[256,4096]{0,1:T(8,128)(2,1)} async-done(((bf16[256,64]{0,1:T(8,128)(2,1)}), bf16[256,4096]{0,1:T(8,128)(2,1)}) %all-gather.9.cloned.1.call-update) | async-done | bytes 2097168 | tf_op jit(solution)/shard_map/all_gather | solution.py:56
  237.7 2.7 fusion.30
  242.2 73.8 %all-gather.11.cloned.1.call-done = bf16[256,4096]{0,1:T(8,128)(2,1)} async-done(((bf16[256,64]{0,1:T(8,128)(2,1)}), bf16[256,4096]{0,1:T(8,128)(2,1)}) %all-gather.11.cloned.1.call-update) | async-done | bytes 2097168 | tf_op jit(solution)/shard_map/all_gather | solution.py:56
  316.1 2.3 fusion.19
  318.4 27.8 %all-gather.13.cloned.1.call-done = bf16[224,4096]{1,0:T(8,128)(2,1)} async-done(((bf16[224,1024]{1,0:T(8,128)(2,1)}), bf16[224,4096]{1,0:T(8,128)(2,1)}) %all-gather.13.cloned.1.call-update) | async-done | bytes 1835024 | tf_op jit(solution)/shard_map/all_gather | solution.py:145
  346.2 2.3 fusion.31
  348.6 30.5 %all-gather.15.cloned.1.call-done = bf16[224,4096]{1,0:T(8,128)(2,1)} async-done(((bf16[224,1024]{1,0:T(8,128)(2,1)}), bf16[224,4096]{1,0:T(8,128)(2,1)}) %all-gather.15.cloned.1.call-update) | async-done | bytes 1835024 | tf_op jit(solution)/shard_map/all_gather | solution.py:146
  379.1 32.9 %all-gather.17.cloned.1.call-done = bf16[224,4096]{1,0:T(8,128)(2,1)} async-done(((bf16[224,1024]{1,0:T(8,128)(2,1)}), bf16[224,4096]{1,0:T(8,128)(2,1)}) %all-gather.17.cloned.1.call-update) | async-done | bytes 1835024 | tf_op jit(solution)/shard_map/all_gather | solution.py:147
  412.0 6.4 %convolution_bitcast_fusion = f32[4096,256]{1,0:T(8,128)} fusion(bf16[224,4096]{1,0:T(8,128)(2,1)} %all-gather.17.cloned.1.call-done, bf16[224,4096]{1,0:T(8,128)(2,1)} %all-gather.15.cloned.1.call-done, bf16[256,4096]{0,1:T(8,128)(2,1)S(1)} %copy-done, f32[4096]{0:T(1024)S(1)} %convert_element_type.105, f32[256]{0:T(256)S(1)} %add_rsqrt_fusion, ...), kind=kOutput, calls=%fused_computation.32 | convolution fusion | flops 944062464 | bytes 10208256 | tf_op jit(solution)/shard_map/dot_general | solution.py:204
  418.4 0.7 compare_and_fusion.2
  420.1 1.3 gather_fusion
  421.4 1.3 gather_fusion.1
  422.8 0.9 fusion.40
  423.7 133.6 %reduce-scatter.2.cloned.1.call-done = f32[64,256]{1,0:T(8,128)} async-done(((f32[4096,256]{1,0:T(8,128)}), f32[64,256]{1,0:T(8,128)}) %reduce-scatter.2.cloned.1.call-update) | async-done | bytes 65552 | tf_op jit(solution)/shard_map/reduce_scatter | solution.py:203
  557.3 1.5 fusion.52
  (119 shorter events, 15.1 us)
Async XLA Ops:
  7.2 85.2 %all-gather.7.cloned.1.call-start = ((), (), s32[]{:S(2)}) async-start(), calls=%async_computation.1 | async-start | bytes 2129920 | tf_op jit(solution)/shard_map/all_gather | solution.py:56
  7.9 229.8 %all-gather.9.cloned.1.call-start = ((), (), s32[]{:S(2)}) async-start(), calls=%async_computation.2 | async-start | bytes 2129920 | tf_op jit(solution)/shard_map/all_gather | solution.py:56
  92.3 2.3 copy-start.1
  95.5 4.3 collective-permute-start
  99.8 4.2 collective-permute-start.1
  104.1 6.9 %collective-permute-start.2 = (bf16[256,384]{0,1:T(8,128)(2,1)S(1)}, bf16[256,384]{0,1:T(8,128)(2,1)S(1)}, u32[]{:S(2)}, u32[]{:S(2)}) collective-permute-start(bf16[256,384]{0,1:T(8,128)(2,1)S(1)} %maximum_select_fusion.1), channel_id=1, source_target_pairs={{0,16},{16,0},{4,20},{20,4},{8,24},{24,8},{12,28},{28,12},{32,48},... | collective-permute-start | bytes 589832 | tf_op jit(solution)/shard_map/ppermute | solution.py:22
  112.1 1.3 copy-start.9
  112.1 1.3 copy-start.11
  121.3 3.3 copy-start.7
  123.2 2.0 copy-start.2
  125.3 4.1 copy-start.4
  130.0 3.6 collective-permute-start.4
  132.1 1.5 collective-permute-start.3
  132.2 1.4 collective-permute-start.9
  133.7 28.4 %copy-start.14 = (bf16[64,1024]{1,0:T(8,128)(2,1)S(1)}, bf16[64,1024]{1,0:T(8,128)(2,1)}, u32[]{:S(2)}) copy-start(bf16[64,1024]{1,0:T(8,128)(2,1)} %param.24) | copy-start | bytes 393220
  133.8 104.0 %copy-start.13 = (bf16[256,64]{0,1:T(8,128)(2,1)S(1)}, bf16[256,64]{0,1:T(8,128)(2,1)}, u32[]{:S(2)}) copy-start(bf16[256,64]{0,1:T(8,128)(2,1)} %param.17) | copy-start | bytes 98308
  133.8 13.4 %collective-permute-start.6 = (f32[256,4,128]{0,2,1:T(8,128)S(1)}, f32[256,4,128]{0,2,1:T(8,128)S(1)}, u32[]{:S(2)}, u32[]{:S(2)}) collective-permute-start(f32[256,4,128]{0,2,1:T(8,128)S(1)} %multiply_add_fusion.3), channel_id=1, source_target_pairs={{0,8},{8,0},{4,12},{12,4},{16,24},{24,16},{20,28},{28,20},{32,40},... | collective-permute-start | bytes 1572872 | tf_op jit(solution)/shard_map/ppermute | solution.py:22
  134.1 13.0 %collective-permute-start.10 = (f32[256,4]{0,1:T(4,128)S(1)}, f32[256,4]{0,1:T(4,128)S(1)}, u32[]{:S(2)}, u32[]{:S(2)}) collective-permute-start(f32[256,4]{0,1:T(4,128)S(1)} %get-tuple-element.243), channel_id=1, source_target_pairs={{0,8},{8,0},{4,12},{12,4},{16,24},{24,16},{20,28},{28,20},{32,40},... | collective-permute-start | bytes 12296 | tf_op jit(solution)/shard_map/ppermute | solution.py:22
  135.3 11.8 %collective-permute-start.5 = (f32[256,4]{0,1:T(4,128)S(1)}, f32[256,4]{0,1:T(4,128)S(1)}, u32[]{:S(2)}, u32[]{:S(2)}) collective-permute-start(f32[256,4]{0,1:T(4,128)S(1)} %get-tuple-element.246), channel_id=1, source_target_pairs={{0,8},{8,0},{4,12},{12,4},{16,24},{24,16},{20,28},{28,20},{32,40},... | collective-permute-start | bytes 12296 | tf_op jit(solution)/shard_map/ppermute | solution.py:22
  147.3 14.0 %collective-permute-start.8 = (f32[256,4,128]{0,2,1:T(8,128)S(1)}, f32[256,4,128]{0,2,1:T(8,128)S(1)}, u32[]{:S(2)}, u32[]{:S(2)}) collective-permute-start(f32[256,4,128]{0,2,1:T(8,128)S(1)} %multiply_add_fusion.2), channel_id=1, source_target_pairs={{0,16},{16,0},{4,20},{20,4},{8,24},{24,8},{12,28},{28,12},{32,48},... | collective-permute-start | bytes 1572872 | tf_op jit(solution)/shard_map/ppermute | solution.py:22
  149.2 11.9 %collective-permute-start.11 = (f32[256,4]{0,1:T(4,128)S(1)}, f32[256,4]{0,1:T(4,128)S(1)}, u32[]{:S(2)}, u32[]{:S(2)}) collective-permute-start(f32[256,4]{0,1:T(4,128)S(1)} %get-tuple-element.239), channel_id=1, source_target_pairs={{0,16},{16,0},{4,20},{20,4},{8,24},{24,8},{12,28},{28,12},{32,48},... | collective-permute-start | bytes 12296 | tf_op jit(solution)/shard_map/ppermute | solution.py:22
  150.3 10.9 %collective-permute-start.7 = (f32[256,4]{0,1:T(4,128)S(1)}, f32[256,4]{0,1:T(4,128)S(1)}, u32[]{:S(2)}, u32[]{:S(2)}) collective-permute-start(f32[256,4]{0,1:T(4,128)S(1)} %get-tuple-element.242), channel_id=1, source_target_pairs={{0,16},{16,0},{4,20},{20,4},{8,24},{24,8},{12,28},{28,12},{32,48},... | collective-permute-start | bytes 12296 | tf_op jit(solution)/shard_map/ppermute | solution.py:22
  162.0 154.1 %all-gather.11.cloned.1.call-start = ((), (), s32[]{:S(2)}) async-start(), calls=%async_computation.3 | async-start | bytes 2129920 | tf_op jit(solution)/shard_map/all_gather | solution.py:56
  172.3 69.9 %copy-start.15 = (bf16[4096]{0:T(1024)(128)(2,1)S(1)}, bf16[4096]{0:T(1024)(128)(2,1)}, u32[]{:S(2)}) copy-start(bf16[4096]{0:T(1024)(128)(2,1)} %param.22) | copy-start | bytes 24580
  240.4 105.8 %all-gather.13.cloned.1.call-start = ((), (), s32[]{:S(2)}) async-start(), calls=%async_computation.4 | async-start | bytes 2293760 | tf_op jit(solution)/shard_map/all_gather | solution.py:145
  241.0 138.1 %all-gather.15.cloned.1.call-start = ((), (), s32[]{:S(2)}) async-start(), calls=%async_computation.5 | async-start | bytes 2293760 | tf_op jit(solution)/shard_map/all_gather | solution.py:146
  241.6 170.4 %all-gather.17.cloned.1.call-start = ((), (), s32[]{:S(2)}) async-start(), calls=%async_computation.6 | async-start | bytes 2293760 | tf_op jit(solution)/shard_map/all_gather | solution.py:147
  242.2 315.1 %reduce-scatter.2.cloned.1.call-start = ((), (), s32[]{:S(2)}) async-start(), calls=%async_computation.7 | async-start | bytes 4259840 | tf_op jit(solution)/shard_map/reduce_scatter | solution.py:203
  316.1 30.1 %copy-start = (bf16[256,4096]{0,1:T(8,128)(2,1)S(1)}, bf16[256,4096]{0,1:T(8,128)(2,1)}, u32[]{:S(2)}) copy-start(bf16[256,4096]{0,1:T(8,128)(2,1)} %all-gather.11.cloned.1.call-done) | copy-start | bytes 6291460
  418.4 1.4 copy-start.3
  418.4 1.6 copy-start.10
  418.4 1.6 copy-start.12
  418.4 4.4 copy-start.5
  418.4 4.4 copy-start.6
  418.4 138.8 %copy-start.8 = (bf16[256,64]{0,1:T(8,128)(2,1)S(1)}, bf16[256,64]{0,1:T(8,128)(2,1)}, u32[]{:S(2)}) copy-start(bf16[256,64]{0,1:T(8,128)(2,1)} %fusion.30) | copy-start | bytes 98308
Sparse Core Ops, SparseCore 0:
  10.8 81.5 all-gather.6
  162.1 75.5 all-gather.8
  241.1 74.9 all-gather.10
  317.7 28.4 all-gather.12
  347.9 31.1 all-gather.14
  380.8 31.1 all-gather.16
  418.5 138.6 reduce-scatter.1
where the time goes:
time: 570 us; the launch traced here: 566 us
  waiting for transfers between devices  460 us (81%)
  other arithmetic  25.7 us (5%)
  blocking collectives  23.4 us (4%)
  between operations  16.5 us (3%)
  matrix products  14.7 us (3%)
  local copies, waits for them, and re-layouts  12.8 us (2%)
  starting transfers between devices  12.1 us (2%)
    all_gather x3, waiting for transfers between devices, gather_cols(): return lax.all_gather(block, 'wide', axis=1, tiled=True)  203 us
    reduce_scatter x1, waiting for transfers between devices, per_device(): lax.psum_scatter(lax.dot_general(down_full, activation, (((0,), (1,)), ((...  134 us
    all_gather x1, waiting for transfers between devices, per_device(): lax.all_gather(wdown, 'narrow', axis=1, tiled=True)  32.9 us
    all_gather x1, waiting for transfers between devices, per_device(): lax.all_gather(wup, 'narrow', axis=1, tiled=True)  30.5 us
    ppermute x12, waiting for transfers between devices, partner(): return lax.ppermute(block, axis, route)  30.3 us
    all_gather x1, waiting for transfers between devices, per_device(): lax.all_gather(wgate, 'narrow', axis=1, tiled=True)  27.8 us
    all_gather x1, blocking collectives, per_device(): lax.all_gather(wqkv, 'narrow', axis=1, tiled=True)  13.1 us
    ppermute x12, starting transfers between devices, partner(): return lax.ppermute(block, axis, route)  11.8 us
  transfers between devices with their start and end apart: 19, of which 14 were waited for; matrix products, arithmetic and copies ran while one was open for 4% of the time, Pallas kernels for 0%

commit v1 on v0

v1 whole, which is shorter than its diff:
```python
import jax
import jax.numpy as jnp
from jax import lax
from jax.experimental import pallas as pl
from jax.experimental.pallas import tpu as pltpu
from jax.sharding import PartitionSpec as P

HD = 128
WINDOW = 4096
NEG_FILL = -1e30
NZ, NY, NX = 8, 4, 4
CHIPS = NZ * NY
TOK = 128
SLOTS = 512
BF16 = jnp.bfloat16
F32 = jnp.float32
YORDER = (0, 1, 3, 2)


def dot(a, b):
    return jnp.dot(a, b, preferred_element_type=F32)


def dot_nt(a, b):
    return lax.dot_general(a, b, (((1,), (1,)), ((), ())), preferred_element_type=F32)


def layer_kernel(
    len_ref, ht, cos, sin, gain1, gain2, kc, vc, wqkv, wo, wg, wu, wd,
    out, nk, nv,
    xb, ab, hb, nb, gq, kvn, krt, ka, vt, sc, sn, ssq,
    wqf, wof, wgf, wuf, wdf, gu, db, ra, rb, sa, sb, ys, yr, fin, fin_r,
    p_s, p_r, ag_s, ag_r, w_l, w_s, w_r, kv_s, kv_r, q_s, q_r, rs_s, rs_r,
):
    wide = lax.axis_index("wide")
    x = lax.axis_index("narrow")
    k = wide % 2
    y = (wide // 2) % NY
    z = wide // (2 * NY)
    sg = 1 - 2 * k
    chip = z * NY + y

    def dev(zz, yy, kk, xx):
        return {"wide": (zz * NY + yy) * 2 + kk, "narrow": xx}

    def ypeer(d):
        return dev(z, (y + d) % NY, k, x)

    partner = dev(z, y, 1 - k, x)
    za = (z + sg + NZ) % NZ
    zb = (z - sg + NZ) % NZ
    dev_a = dev(za, y, k, x)
    dev_b = dev(zb, y, k, x)
    xr = (x + 1) % NX
    xl = (x + NX - 1) % NX
    xo = (x + 2) % NX
    dev_xr = dev(z, y, k, xr)
    dev_xl = dev(z, y, k, xl)

    pending = []

    def send(src, dst, s_sem, r_sem, device):
        copy = pltpu.make_async_remote_copy(
            src_ref=src, dst_ref=dst, send_sem=s_sem, recv_sem=r_sem,
            device_id=device, device_id_type=pl.DeviceIdType.MESH,
        )
        copy.start()
        pending.append(copy)

    def arrive(dst, r_sem):
        pltpu.make_async_remote_copy(
            src_ref=dst, dst_ref=dst, send_sem=r_sem, recv_sem=r_sem,
            device_id=partner, device_id_type=pl.DeviceIdType.MESH,
        ).wait_recv()

    barrier = pltpu.get_barrier_semaphore()
    greet = [partner, ypeer(1), ypeer(2), ypeer(3), dev_a, dev_b, dev_xr, dev_xl]
    for peer in greet:
        pl.semaphore_signal(barrier, inc=1, device_id=peer, device_id_type=pl.DeviceIdType.MESH)
    vt[2 * y + k] = jnp.transpose(vc[...].astype(F32)).astype(BF16)
    ka[2 * y + k] = kc[...]
    ssq[...] = jnp.zeros_like(ssq)
    pl.semaphore_wait(barrier, len(greet))

    own_w = (wqkv, wo, wg, wu, wd)
    full_w = (wqf, wof, wgf, wuf, wdf)
    locals_w = []

    def w_first(m):
        f, o = full_w[m], own_w[m]
        copy = pltpu.make_async_copy(o, f.at[x, k], w_l.at[m])
        copy.start()
        locals_w.append(copy)
        send(o, f.at[x, k], w_s.at[m, 0], w_r.at[m, 0], dev_xr)
        send(o, f.at[x, k], w_s.at[m, 1], w_r.at[m, 1], dev_xl)
        send(o, f.at[x, k], w_s.at[m, 4], w_r.at[m, 4], partner)

    def w_second(m):
        f = full_w[m]
        half = f.shape[2] // 2
        lo, hi = pl.ds(0, half), pl.ds(half, half)
        arrive(f.at[xl, k], w_r.at[m, 0])
        send(f.at[xl, k, lo], f.at[xl, k, lo], w_s.at[m, 2], w_r.at[m, 2], dev_xr)
        send(f.at[xl, k], f.at[xl, k], w_s.at[m, 5], w_r.at[m, 5], partner)
        arrive(f.at[xr, k], w_r.at[m, 1])
        send(f.at[xr, k, hi], f.at[xr, k, hi], w_s.at[m, 3], w_r.at[m, 3], dev_xl)
        send(f.at[xr, k], f.at[xr, k], w_s.at[m, 6], w_r.at[m, 6], partner)

    def w_third(m):
        f = full_w[m]
        half = f.shape[2] // 2
        lo, hi = pl.ds(0, half), pl.ds(half, half)
        arrive(f.at[xo, k, lo], w_r.at[m, 2])
        arrive(f.at[xo, k, hi], w_r.at[m, 3])
        send(f.at[xo, k], f.at[xo, k], w_s.at[m, 7], w_r.at[m, 7], partner)

    def w_ready(m):
        f = full_w[m]
        locals_w[m].wait()
        for i, block in enumerate((x, xl, xr, xo)):
            arrive(f.at[block, 1 - k], w_r.at[m, 4 + i])

    def all_gather(g, buf, on_chunk, extra, pumps):
        send_sem, recv_sem = ag_s.at[g], ag_r.at[g]

        def a_sem(s, d):
            return 3 + (s - 1) * 4 + d

        def b_sem(s, d):
            return 19 + (s - 1) * 4 + d

        def row(zz, d):
            return ((zz + 2 * NZ) % NZ) * NY + (y + NY - d) % NY

        def push_a(s, d):
            ref = buf.at[row(z - sg * (s - 1), d)]
            send(ref, ref, send_sem.at[a_sem(s, d)], recv_sem.at[a_sem(s, d)], dev_a)

        def push_b(s, d):
            ref = buf.at[row(z + sg * (s - 1), d)]
            send(ref, ref, send_sem.at[b_sem(s, d)], recv_sem.at[b_sem(s, d)], dev_b)

        own = buf.at[chip]
        for d in (1, 3, 2):
            send(own, own, send_sem.at[d - 1], recv_sem.at[d - 1], ypeer(d))
        push_a(1, 0)
        push_b(1, 0)
        extra()
        on_chunk(chip)
        for d in YORDER[1:]:
            arrive(buf.at[row(z, d)], recv_sem.at[d - 1])
            push_a(1, d)
            push_b(1, d)
            on_chunk(row(z, d))
        for s in range(2, 6):
            for d in YORDER:
                c = row(z - sg * (s - 1), d)
                arrive(buf.at[c], recv_sem.at[a_sem(s - 1, d)])
                if s <= 4:
                    push_a(s, d)
                on_chunk(c)
                if s <= 4:
                    c = row(z + sg * (s - 1), d)
                    arrive(buf.at[c], recv_sem.at[b_sem(s - 1, d)])
                    if s <= 3:
                        push_b(s, d)
                    on_chunk(c)
            if s in pumps:
                pumps[s]()

    def add_square(buf):
        def run(c):
            v = buf[c].astype(F32)
            ssq[...] += jnp.sum((v * v).reshape(16, 8, TOK), axis=0)

        return run

    def normalise(buf, gain):
        mean_square = jnp.sum(ssq[...], axis=0, keepdims=True) * (1.0 / (CHIPS * 128))
        r = lax.rsqrt(mean_square + 1e-05)
        gains = gain[...]
        for c in range(CHIPS):
            nb[c] = (buf[c].astype(F32) * r * gains[:, c : c + 1]).astype(BF16)

    half_rows = pl.ds(pl.multiple_of(k * 64, 64), 64)
    other_rows = pl.ds(pl.multiple_of((1 - k) * 64, 64), 64)
    send(ht.at[1 - k], xb.at[chip, half_rows], p_s.at[0], p_r.at[0], partner)
    xb[chip, half_rows, :] = ht[k]
    w_first(0)
    w_first(1)
    arrive(xb.at[chip, other_rows], p_r.at[0])

    def send_caches():
        p = 2 * y + k
        for d in (1, 3, 2):
            send(ka.at[p], ka.at[p], kv_s.at[0, d - 1], kv_r.at[0, d - 1], ypeer(d))
            send(vt.at[p], vt.at[p], kv_s.at[1, d - 1], kv_r.at[1, d - 1], ypeer(d))
        send(ka.at[p], ka.at[p], kv_s.at[0, 3], kv_r.at[0, 3], partner)
        send(vt.at[p], vt.at[p], kv_s.at[1, 3], kv_r.at[1, 3], partner)

    def pass_caches():
        for d in (1, 3, 2):
            p = 2 * ((y + NY - d) % NY) + k
            for i, buf in enumerate((ka, vt)):
                arrive(buf.at[p], kv_r.at[i, d - 1])
                send(buf.at[p], buf.at[p], kv_s.at[i, 3 + d], kv_r.at[i, 3 + d], partner)

    def caches_ready():
        for d in range(NY):
            p = 2 * ((y + NY - d) % NY) + 1 - k
            for i, buf in enumerate((ka, vt)):
                arrive(buf.at[p], kv_r.at[i, 3 + d])

    def pump_first():
        w_second(0)
        w_first(2)

    all_gather(
        0, xb, add_square(xb), send_caches,
        {3: pump_first, 5: lambda: w_third(0)},
    )
    normalise(xb, gain1)
    w_ready(0)
    rows_q = wqf.shape[2] * 2
    acc = jnp.zeros((rows_q, TOK), F32)
    for i in range(NX):
        acc += dot(wqf[i].reshape(rows_q, 1024), nb[8 * i : 8 * i + 8].reshape(1024, TOK))
    gq[y] = acc.astype(BF16)

    for d in (1, 3, 2):
        send(gq.at[y], gq.at[y], q_s.at[d - 1], q_r.at[d - 1], ypeer(d))
    w_second(1)
    w_first(3)
    pass_caches()
    for d in (1, 3, 2):
        arrive(gq.at[(y + NY - d) % NY], q_r.at[d - 1])
    grouped = gq[...].reshape(NY * rows_q, TOK)
    kvn[k] = grouped[4 * HD :]
    send(kvn.at[k], kvn.at[k], q_s.at[3], q_r.at[3], partner)

    def rotate(v, cosine, sine):
        v = v.astype(F32)
        a, b = v[:64], v[64:]
        return jnp.concatenate([a * cosine - b * sine, b * cosine + a * sine], axis=0)

    sn[...] = jnp.zeros_like(sn)
    for head in range(NY):

        @pl.when(y == head)
        def _():
            sn[0] = rotate(grouped[head * HD : (head + 1) * HD], cos[k], sin[k])

    qt = sn[0].astype(BF16)
    length = len_ref[x]
    t_row = lax.broadcasted_iota(jnp.int32, (1, TOK), 1) + TOK * k
    caches_ready()

    def cache_scores(b, peak):
        s = dot(ka[b], qt) * HD ** (-0.5)
        slot = lax.broadcasted_iota(jnp.int32, (SLOTS, 1), 0) + b * SLOTS
        allowed = (slot < length) & (slot > length + t_row - WINDOW)
        s = jnp.where(allowed, s, NEG_FILL)
        sc[b] = s
        return jnp.maximum(peak, jnp.max(s, axis=0, keepdims=True))

    peak = lax.fori_loop(0, WINDOW // SLOTS, cache_scores, jnp.full((1, TOK), NEG_FILL, F32))
    arrive(kvn.at[1 - k], q_r.at[3])
    for h in range(2):
        kt = rotate(kvn[h, :HD], cos[h], sin[h])
        krt[h] = kt.astype(BF16)
        s = dot(jnp.transpose(kt).astype(BF16), qt) * HD ** (-0.5)
        t2 = lax.broadcasted_iota(jnp.int32, (TOK, 1), 0) + TOK * h
        s = jnp.where(t2 <= t_row, s, NEG_FILL)
        sn[h] = s
        peak = jnp.maximum(peak, jnp.max(s, axis=0, keepdims=True))

    def cache_mix(b, carry):
        total, mixed = carry
        e = jnp.exp(sc[b] - peak)
        return (total + jnp.sum(e, axis=0, keepdims=True), mixed + dot(vt[b], e.astype(BF16)))

    total, mixed = lax.fori_loop(
        0, WINDOW // SLOTS, cache_mix, (jnp.zeros((1, TOK), F32), jnp.zeros((HD, TOK), F32))
    )
    for h in range(2):
        e = jnp.exp(sn[h] - peak)
        total = total + jnp.sum(e, axis=0, keepdims=True)
        mixed = mixed + dot(kvn[h, HD:], e.astype(BF16))
    ab[chip] = (mixed / total).astype(BF16)

    def update_caches():
        slot = lax.broadcasted_iota(jnp.int32, (SLOTS, TOK), 0) + (2 * y + k) * SLOTS
        offset = slot - length
        offset = jnp.where(offset < 0, offset + WINDOW, offset)
        lane = lax.broadcasted_iota(jnp.int32, (SLOTS, TOK), 1)
        first = jnp.where(offset == lane, 1.0, 0.0).astype(BF16)
        second = jnp.where(offset == lane + TOK, 1.0, 0.0).astype(BF16)
        fresh = offset < 2 * TOK
        keys = dot_nt(first, krt[0]) + dot_nt(second, krt[1])
        vals = dot_nt(first, kvn[0, HD:]) + dot_nt(second, kvn[1, HD:])
        nk[...] = jnp.where(fresh, keys, kc[...].astype(F32)).astype(BF16)
        nv[...] = jnp.where(fresh, vals, vc[...].astype(F32)).astype(BF16)

    def before_second():
        w_second(2)
        w_first(4)
        w_third(1)
        update_caches()

    all_gather(
        1, ab, lambda c: None, before_second,
        {3: lambda: w_second(3), 5: lambda: w_third(2)},
    )
    w_ready(1)
    rows_o = wof.shape[2] * 2
    acc = xb[chip].astype(F32)
    proj = jnp.zeros((rows_o, TOK), F32)
    for i in range(NX):
        proj += dot(wof[i].reshape(rows_o, 1024), ab[8 * i : 8 * i + 8].reshape(1024, TOK))
    hb[chip] = (acc + proj).astype(BF16)
    ssq[...] = jnp.zeros_like(ssq)

    all_gather(
        2, hb, add_square(hb), lambda: w_second(4),
        {4: lambda: w_third(3)},
    )
    normalise(hb, gain2)
    w_ready(2)
    w_ready(3)
    rows_f = wgf.shape[2] * 2
    gu[...] = jnp.zeros_like(gu)

    def hidden_step(i, carry):
        block = nb[pl.ds(pl.multiple_of(8 * i, 8), 8)].reshape(1024, TOK)
        gu[0] += dot(wgf[i].reshape(rows_f, 1024), block)
        gu[1] += dot(wuf[i].reshape(rows_f, 1024), block)
        return carry

    lax.fori_loop(0, NX, hidden_step, 0)
    gate = gu[0]
    act = (gate / (1.0 + jnp.exp(-gate))) * gu[1]
    act_t = jnp.transpose(act).astype(BF16)
    w_third(4)
    w_ready(4)

    def down(r):
        zz = (z + sg * r + 2 * NZ) % NZ
        cols = pl.ds(pl.multiple_of((zz % 2) * 512, 512), 512)
        part = dot(act_t, wdf[zz // 2, :, :, cols].reshape(rows_f, 512))
        for j in range(NY):
            db[zz * NY + j] = part[:, j * 128 : (j + 1) * 128]

    def plane_row(r, d):
        return ((z + sg * r + 2 * NZ) % NZ) * NY + (y + NY - d) % NY

    def sum_a(s, d):
        v = db[plane_row(5 - s, d)]
        if s > 1:
            arrive(ra.at[s - 2, d], rs_r.at[3 + (s - 2) * 4 + d])
            v = v + ra[s - 2, d].astype(F32)
        sa[s - 1, d] = v.astype(BF16)
        i = 3 + (s - 1) * 4 + d
        send(sa.at[s - 1, d], ra.at[s - 1, d], rs_s.at[i], rs_r.at[i], dev_a)

    def sum_b(s, d):
        v = db[plane_row(s - 4, d)]
        if s > 1:
            arrive(rb.at[s - 2, d], rs_r.at[19 + (s - 2) * 4 + d])
            v = v + rb[s - 2, d].astype(F32)
        sb[s - 1, d] = v.astype(BF16)
        i = 19 + (s - 1) * 4 + d
        send(sb.at[s - 1, d], rb.at[s - 1, d], rs_s.at[i], rs_r.at[i], dev_b)

    down(4)
    for d in (2, 1, 3, 0):
        sum_a(1, d)
    down(-3)
    for d in (2, 1, 3, 0):
        sum_b(1, d)

    def down_step(i, carry):
        down(jnp.where(i % 2 == 0, 3 - i // 2, i // 2 - 2))
        return carry

    lax.fori_loop(0, 6, down_step, 0)
    for s in (2, 3, 4):
        for d in (2, 1, 3, 0):
            sum_a(s, d)
            if s <= 3:
                sum_b(s, d)
    whole = None
    for d in (2, 1, 3, 0):
        arrive(rb.at[2, d], rs_r.at[19 + 8 + d])
        arrive(ra.at[3, d], rs_r.at[3 + 12 + d])
        v = db[plane_row(0, d)] + ra[3, d].astype(F32) + rb[2, d].astype(F32)
        if d == 0:
            whole = v
        else:
            ys[d - 1] = v.astype(BF16)
            send(ys.at[d - 1], yr.at[d - 1], rs_s.at[d - 1], rs_r.at[d - 1], ypeer(NY - d))
    for d in (1, 3, 2):
        arrive(yr.at[d - 1], rs_r.at[d - 1])
        whole = whole + yr[d - 1].astype(F32)
    fin[...] = (hb[chip].astype(F32) + jnp.transpose(whole)).astype(BF16)
    send(fin.at[other_rows], fin_r, rs_s.at[31], rs_r.at[31], partner)
    out[k] = fin[half_rows, :]
    arrive(fin_r, rs_r.at[31])
    out[1 - k] = fin_r[...]
    for copy in pending:
        copy.wait_send()


def per_device(
    hidden_in, cached_len, k_cache, v_cache, attn_gain, ffn_gain, wqkv, wo, wgate, wup, wdown
):
    ht = hidden_in.reshape(2, TOK, 64).transpose(0, 2, 1)
    length = cached_len[lax.axis_index("narrow")]
    exponent = jnp.arange(HD // 2, dtype=F32) * (2.0 / HD)
    frequency = jnp.power(10000.0, -exponent)
    positions = (length + jnp.arange(2 * TOK, dtype=jnp.int32)).astype(F32).reshape(2, 1, TOK)
    angles = positions * frequency[None, :, None]
    gain1 = attn_gain.astype(F32).reshape(CHIPS, 128).T
    gain2 = ffn_gain.astype(F32).reshape(CHIPS, 128).T

    def vm(*shape, dtype=BF16):
        return pltpu.VMEM(shape, dtype)

    def sems(*shape):
        return pltpu.SemaphoreType.DMA(shape)

    def full(w):
        return vm(NX, 2, w.shape[0], w.shape[1])

    in_vmem = pl.BlockSpec(memory_space=pltpu.VMEM)
    in_hbm = pl.BlockSpec(memory_space=pl.ANY)
    out, nk, nv = pl.pallas_call(
        layer_kernel,
        out_shape=(
            jax.ShapeDtypeStruct((2, 64, TOK), BF16),
            jax.ShapeDtypeStruct((SLOTS, HD), BF16),
            jax.ShapeDtypeStruct((SLOTS, HD), BF16),
        ),
        in_specs=[pl.BlockSpec(memory_space=pltpu.SMEM)] + [in_vmem] * 7 + [in_hbm] * 5,
        out_specs=(in_vmem, in_vmem, in_vmem),
        scratch_shapes=[
            vm(CHIPS, 128, TOK), vm(CHIPS, 128, TOK), vm(CHIPS, 128, TOK), vm(CHIPS, 128, TOK),
            vm(NY, 2 * wqkv.shape[0], TOK), vm(2, 2 * HD, TOK), vm(2, HD, TOK),
            vm(8, SLOTS, HD), vm(8, HD, SLOTS),
            vm(8, SLOTS, TOK, dtype=F32), vm(2, TOK, TOK, dtype=F32), vm(8, TOK, dtype=F32),
            full(wqkv), full(wo), full(wgate), full(wup), full(wdown),
            vm(2, 2 * wgate.shape[0], TOK, dtype=F32),
            vm(CHIPS, TOK, 128, dtype=F32),
            vm(4, NY, TOK, 128), vm(3, NY, TOK, 128), vm(4, NY, TOK, 128), vm(3, NY, TOK, 128),
            vm(3, TOK, 128), vm(3, TOK, 128), vm(128, TOK), vm(64, TOK),
            sems(1), sems(1), sems(3, 31), sems(3, 31), sems(5), sems(5, 8), sems(5, 8),
            sems(2, 7), sems(2, 7), sems(4), sems(4), sems(32), sems(32),
        ],
        compiler_params=pltpu.CompilerParams(
            collective_id=0, has_side_effects=True, vmem_limit_bytes=60 * 1024 * 1024
        ),
        name="layer",
    )(
        cached_len, ht, jnp.cos(angles), jnp.sin(angles), gain1, gain2,
        k_cache[0], v_cache[0], wqkv, wo, wgate, wup, wdown,
    )
    hidden_out = out.transpose(0, 2, 1).reshape(2 * TOK, 64)
    return (hidden_out, nk[None], nv[None])


def solution(mesh):
    return jax.shard_map(
        per_device,
        mesh=mesh,
        in_specs=(
            P("narrow", "wide"),
            P(),
            P("narrow", "wide", None),
            P("narrow", "wide", None),
            P(),
            P(),
            P("wide", "narrow"),
            P("wide", "narrow"),
            P("wide", "narrow"),
            P("wide", "narrow"),
            P("wide", "narrow"),
        ),
        out_specs=(P("narrow", "wide"), P("narrow", "wide", None), P("narrow", "wide", None)),
        check_vma=False,
    )
```

time: 570 us -> 116 us (0.20)
  waiting for transfers between devices: 460 us -> 0 us
  Pallas kernels: 0 us -> 105 us
  other arithmetic: 25.7 us -> 1.63 us
  blocking collectives: 23.4 us -> 0 us
  between operations: 16.5 us -> 0.7 us
  matrix products: 14.7 us -> 0 us
  starting transfers between devices: 12.1 us -> 0 us
    all_gather x6 -> x0, waiting for transfers between devices: 294 us -> none  [the longest x3 203 us: gather_cols(): return lax.all_gather(block, 'wide', axis=1, tiled=True)]
    reduce_scatter x1 -> x0, waiting for transfers between devices: 134 us -> none  [per_device(): lax.psum_scatter(lax.dot_general(down_full, activation, (((0,), (1,)), ((...]
    pallas_call x0 -> x1, Pallas kernels: none -> 105 us  [per_device(): pl.pallas_call(layer_kernel, out_shape=(jax.ShapeDtypeStruct((2, 64, TOK)...]
    ppermute x12 -> x0, waiting for transfers between devices: 30.3 us -> none  [partner(): return lax.ppermute(block, axis, route)]
    all_gather x2 -> x0, blocking collectives: 23.4 us -> none  [the longest x1 13.1 us: per_device(): lax.all_gather(wqkv, 'narrow', axis=1, tiled=True)]
    dot_general x8 -> x0, matrix products: 14.7 us -> none  [the longest x1 6.36 us: per_device(): lax.dot_general(down_full, activation, (((0,), (1,)), ((), ())), preferre...]
    ppermute x12 -> x0, starting transfers between devices: 11.8 us -> none  [partner(): return lax.ppermute(block, axis, route)]
  transfers between devices with their start and end apart: 19 -> 0, of which waited for: 14 -> 0; matrix products, arithmetic and copies ran while one was open for 4% -> 0% of each run, Pallas kernels for 0% -> 0%
where the time goes in v1:
time: 116 us; the launch traced here: 115 us
  Pallas kernels  105 us (91%)
  local copies, waits for them, and re-layouts  7.63 us (7%)
  other arithmetic  1.63 us (1%)
    pallas_call x1, Pallas kernels, per_device(): pl.pallas_call(layer_kernel, out_shape=(jax.ShapeDtypeStruct((2, 64, TOK)...  105 us
    unnamed x12, local copies, waits for them, and re-layouts  3.6 us

profile of v1, /device:TPU:1, one launch (start us, length us, event | category | flops | bytes accessed | tf_op | source)
XLA Modules:
  0.0 115.3 jit_solution(2733900499524086693)
XLA Ops:
  0.6 0.0 copy-start
  0.6 0.0 copy-start.4
  0.7 0.0 copy-start.2
  0.7 0.6 copy-done.4
  1.3 0.6 dynamic_slice.3
  1.9 0.7 add_convert_fusion
  2.6 0.0 copy-done.2
  2.6 0.0 copy-start.3
  2.6 0.7 copy-done.3
  3.3 0.0 copy-done
  3.3 0.6 bitcast_bitcast_fusion.ht
  3.9 0.7 copy.16
  4.6 0.7 copy.15
  5.3 1.0 multiply_sine_fusion
  6.3 105.3 %layer.1 = (bf16[2,64,128]{2,1,0:T(8,128)(2,1)}, bf16[512,128]{1,0:T(8,128)(2,1)}, bf16[512,128]{1,0:T(8,128)(2,1)}) custom-call(s32[4]{0:T(128)} %len_ref.1, bf16[2,64,128]{2,1,0:T(8,128)(2,1)} %bitcast_bitcast_fusion.ht, f32[2,64,128]{2,1,0:T(8,128)} %get-tuple-element.10.cos, f32[2,64,128]{2,1,0:T(8,128)} %get-tuple-element.9.sin, f32[128,32]{1,0:T(8,128)} %bitcast.27, ...), custom_call_target="tpu_custom_call" | custom-call | tf_op jit(solution)/shard_map/layer/pallas_call | solution.py:436
  111.6 1.4 %copy_bitcast_fusion = bf16[256,64]{0,1:T(8,128)(2,1)} fusion(bf16[2,64,128]{2,1,0:T(8,128)(2,1)} %get-tuple-element.6), kind=kLoop, calls=%fused_computation.2 | loop fusion | bytes 65536 | tf_op jit(solution)/shard_map/reshape | solution.py:466
  113.0 0.0 copy-start.1
  113.0 1.6 %copy.24 = bf16[1,512,128]{2,1,0:T(8,128)(2,1)} copy(bf16[1,512,128]{2,1,0:T(8,128)(2,1)} %bitcast.31) | data formatting | bytes 262144
  114.6 0.0 copy-done.1
  114.6 0.7 copy.25
  (3 shorter events, 0.0 us)
Async XLA Ops:
  0.6 2.6 %copy-start = (bf16[256,64]{0,1:T(8,128)(2,1)S(1)}, bf16[256,64]{0,1:T(8,128)(2,1)}, u32[]{:S(2)}) copy-start(bf16[256,64]{0,1:T(8,128)(2,1)} %param.11) | copy-start | bytes 98308
  0.6 0.7 copy-start.4
  0.7 1.9 %copy-start.2 = (bf16[4096]{0:T(1024)(128)(2,1)S(1)}, bf16[4096]{0:T(1024)(128)(2,1)}, u32[]{:S(2)}) copy-start(bf16[4096]{0:T(1024)(128)(2,1)} %param.15) | copy-start | bytes 24580
  2.6 0.7 copy-start.3
  113.0 1.6 %copy-start.1 = (bf16[512,128]{1,0:T(8,128)(2,1)S(1)}, bf16[512,128]{1,0:T(8,128)(2,1)}, u32[]{:S(2)}) copy-start(bf16[512,128]{1,0:T(8,128)(2,1)} %get-tuple-element.8) | copy-start | bytes 393220

commit v2 on v1

--- a/solution.py
+++ b/solution.py
@@ -1,5 +1,6 @@
 import jax
 import jax.numpy as jnp
+import numpy as np
 from jax import lax
 from jax.experimental import pallas as pl
 from jax.experimental.pallas import tpu as pltpu
@@ -15,6 +16,8 @@
 BF16 = jnp.bfloat16
 F32 = jnp.float32
 YORDER = (0, 1, 3, 2)
+NEAR = (1, -1, 2, -2, 3, -3, 4)
+FAR = (4, 3, -3, 2, -2, 1, -1, 0)
 
 
 def dot(a, b):
@@ -26,10 +29,10 @@
 
 
 def layer_kernel(
-    len_ref, ht, cos, sin, gain1, gain2, kc, vc, wqkv, wo, wg, wu, wd,
+    len_ref, hid, freq, gain1, gain2, kc, vc, wqkv, wo, wg, wu, wd,
     out, nk, nv,
-    xb, ab, hb, nb, gq, kvn, krt, ka, vt, sc, sn, ssq,
-    wqf, wof, wgf, wuf, wdf, gu, db, ra, rb, sa, sb, ys, yr, fin, fin_r,
+    ht, cos, sin, xb, ab, hb, nb, gq, kvn, krt, ka, vt, sc, sn, ssq,
+    wqf, wof, wgf, wuf, wdf, gu, db, ys, yr, zs, zr, fin, fin_r,
     p_s, p_r, ag_s, ag_r, w_l, w_s, w_r, kv_s, kv_r, q_s, q_r, rs_s, rs_r,
 ):
     wide = lax.axis_index("wide")
@@ -45,6 +48,9 @@
 
     def ypeer(d):
         return dev(z, (y + d) % NY, k, x)
+
+    def zpeer(d):
+        return dev((z + d + NZ) % NZ, y, k, x)
 
     partner = dev(z, y, 1 - k, x)
     za = (z + sg + NZ) % NZ
@@ -74,9 +80,11 @@
         ).wait_recv()
 
     barrier = pltpu.get_barrier_semaphore()
-    greet = [partner, ypeer(1), ypeer(2), ypeer(3), dev_a, dev_b, dev_xr, dev_xl]
+    greet = [partner, ypeer(1), ypeer(2), ypeer(3), dev_xr, dev_xl] + [zpeer(d) for d in NEAR]
     for peer in greet:
         pl.semaphore_signal(barrier, inc=1, device_id=peer, device_id_type=pl.DeviceIdType.MESH)
+    for h in range(2):
+        ht[h] = hid[:, h * TOK : (h + 1) * TOK]
     vt[2 * y + k] = jnp.transpose(vc[...].astype(F32)).astype(BF16)
     ka[2 * y + k] = kc[...]
     ssq[...] = jnp.zeros_like(ssq)
@@ -168,6 +176,37 @@
             if s in pumps:
                 pumps[s]()
 
+    def all_gather_direct(g, buf, on_chunk, extra, pumps):
+        send_sem, recv_sem = ag_s.at[g], ag_r.at[g]
+
+        def row(dz, dy):
+            return ((z + dz + NZ) % NZ) * NY + (y + dy + NY) % NY
+
+        def y_sem(dz, d):
+            return 8 + (dz % NZ) * 3 + d - 1
+
+        def y_send(dz):
+            ref = buf.at[row(dz, 0)]
+            for d in (2, 1, 3):
+                send(ref, ref, send_sem.at[y_sem(dz, d)], recv_sem.at[y_sem(dz, d)], ypeer(d))
+
+        own = buf.at[chip]
+        for dz in NEAR:
+            send(own, own, send_sem.at[dz % NZ], recv_sem.at[dz % NZ], zpeer(dz))
+        y_send(0)
+        extra()
+        on_chunk(chip)
+        for dz in NEAR:
+            arrive(buf.at[row(-dz, 0)], recv_sem.at[dz % NZ])
+            y_send(-dz)
+            on_chunk(row(-dz, 0))
+        for i, dz in enumerate((0,) + NEAR):
+            for d in (1, 3, 2):
+                arrive(buf.at[row(-dz, -d)], recv_sem.at[y_sem(-dz, d)])
+                on_chunk(row(-dz, -d))
+            if i in pumps:
+                pumps[i]()
+
     def add_square(buf):
         def run(c):
             v = buf[c].astype(F32)
@@ -178,7 +217,7 @@
     def normalise(buf, gain):
         mean_square = jnp.sum(ssq[...], axis=0, keepdims=True) * (1.0 / (CHIPS * 128))
         r = lax.rsqrt(mean_square + 1e-05)
-        gains = gain[...]
+        gains = jnp.transpose(gain[...].astype(F32))
         for c in range(CHIPS):
             nb[c] = (buf[c].astype(F32) * r * gains[:, c : c + 1]).astype(BF16)
 
@@ -211,12 +250,20 @@
             for i, buf in enumerate((ka, vt)):
                 arrive(buf.at[p], kv_r.at[i, 3 + d])
 
+    def before_first():
+        send_caches()
+        for h in range(2):
+            t = lax.broadcasted_iota(jnp.int32, (1, TOK), 1) + (TOK * h + len_ref[x])
+            angle = freq[:, 0:1] * t.astype(F32)
+            cos[h] = jnp.cos(angle)
+            sin[h] = jnp.sin(angle)
+
     def pump_first():
         w_second(0)
         w_first(2)
 
     all_gather(
-        0, xb, add_square(xb), send_caches,
+        0, xb, add_square(xb), before_first,
         {3: pump_first, 5: lambda: w_third(0)},
     )
     normalise(xb, gain1)
@@ -307,9 +354,9 @@
         w_third(1)
         update_caches()
 
-    all_gather(
+    all_gather_direct(
         1, ab, lambda c: None, before_second,
-        {3: lambda: w_second(3), 5: lambda: w_third(2)},
+        {4: lambda: w_second(3), 7: lambda: w_third(2)},
     )
     w_ready(1)
     rows_o = wof.shape[2] * 2
@@ -320,9 +367,9 @@
     hb[chip] = (acc + proj).astype(BF16)
     ssq[...] = jnp.zeros_like(ssq)
 
-    all_gather(
-        2, hb, add_square(hb), lambda: w_second(4),
-        {4: lambda: w_third(3)},
+    all_gather_direct(
+        2, hb, add_square(hb), lambda: None,
+        {3: lambda: w_second(4), 7: lambda: w_third(3)},
     )
     normalise(hb, gain2)
     w_ready(2)
@@ -343,69 +390,35 @@
     w_third(4)
     w_ready(4)
 
-    def down(r):
-        zz = (z + sg * r + 2 * NZ) % NZ
+    for i, r in enumerate(FAR):
+        zz = (z + r + NZ) % NZ
         cols = pl.ds(pl.multiple_of((zz % 2) * 512, 512), 512)
-        part = dot(act_t, wdf[zz // 2, :, :, cols].reshape(rows_f, 512))
-        for j in range(NY):
-            db[zz * NY + j] = part[:, j * 128 : (j + 1) * 128]
-
-    def plane_row(r, d):
-        return ((z + sg * r + 2 * NZ) % NZ) * NY + (y + NY - d) % NY
-
-    def sum_a(s, d):
-        v = db[plane_row(5 - s, d)]
-        if s > 1:
-            arrive(ra.at[s - 2, d], rs_r.at[3 + (s - 2) * 4 + d])
-            v = v + ra[s - 2, d].astype(F32)
-        sa[s - 1, d] = v.astype(BF16)
-        i = 3 + (s - 1) * 4 + d
-        send(sa.at[s - 1, d], ra.at[s - 1, d], rs_s.at[i], rs_r.at[i], dev_a)
-
-    def sum_b(s, d):
-        v = db[plane_row(s - 4, d)]
-        if s > 1:
-            arrive(rb.at[s - 2, d], rs_r.at[19 + (s - 2) * 4 + d])
-            v = v + rb[s - 2, d].astype(F32)
-        sb[s - 1, d] = v.astype(BF16)
-        i = 19 + (s - 1) * 4 + d
-        send(sb.at[s - 1, d], rb.at[s - 1, d], rs_s.at[i], rs_r.at[i], dev_b)
-
-    down(4)
-    for d in (2, 1, 3, 0):
-        sum_a(1, d)
-    down(-3)
-    for d in (2, 1, 3, 0):
-        sum_b(1, d)
-
-    def down_step(i, carry):
-        down(jnp.where(i % 2 == 0, 3 - i // 2, i // 2 - 2))
-        return carry
-
-    lax.fori_loop(0, 6, down_step, 0)
-    for s in (2, 3, 4):
-        for d in (2, 1, 3, 0):
-            sum_a(s, d)
-            if s <= 3:
-                sum_b(s, d)
+        db[i] = dot(act_t, wdf[zz // 2, :, :, cols].reshape(rows_f, 512))
+        for d in (2, 1, 3):
+            col = pl.ds(pl.multiple_of(((y + d) % NY) * 128, 128), 128)
+            ys[i, d - 1] = db[i, :, col].astype(BF16)
+            n = 3 * i + d - 1
+            send(ys.at[i, d - 1], yr.at[i, d - 1], rs_s.at[n], rs_r.at[n], ypeer(d))
+    own_col = pl.ds(pl.multiple_of(y * 128, 128), 128)
     whole = None
-    for d in (2, 1, 3, 0):
-        arrive(rb.at[2, d], rs_r.at[19 + 8 + d])
-        arrive(ra.at[3, d], rs_r.at[3 + 12 + d])
-        v = db[plane_row(0, d)] + ra[3, d].astype(F32) + rb[2, d].astype(F32)
-        if d == 0:
+    for i, r in enumerate(FAR):
+        v = db[i, :, own_col]
+        for d in (1, 3, 2):
+            arrive(yr.at[i, d - 1], rs_r.at[3 * i + d - 1])
+            v = v + yr[i, d - 1].astype(F32)
+        if r == 0:
             whole = v
         else:
-            ys[d - 1] = v.astype(BF16)
-            send(ys.at[d - 1], yr.at[d - 1], rs_s.at[d - 1], rs_r.at[d - 1], ypeer(NY - d))
-    for d in (1, 3, 2):
-        arrive(yr.at[d - 1], rs_r.at[d - 1])
-        whole = whole + yr[d - 1].astype(F32)
+            zs[i] = v.astype(BF16)
+            send(zs.at[i], zr.at[i], rs_s.at[24 + i], rs_r.at[24 + i], zpeer(r))
+    for i in reversed(range(NZ - 1)):
+        arrive(zr.at[i], rs_r.at[24 + i])
+        whole = whole + zr[i].astype(F32)
     fin[...] = (hb[chip].astype(F32) + jnp.transpose(whole)).astype(BF16)
     send(fin.at[other_rows], fin_r, rs_s.at[31], rs_r.at[31], partner)
-    out[k] = fin[half_rows, :]
+    out[:, pl.ds(pl.multiple_of(k * TOK, TOK), TOK)] = fin[half_rows, :]
     arrive(fin_r, rs_r.at[31])
-    out[1 - k] = fin_r[...]
+    out[:, pl.ds(pl.multiple_of((1 - k) * TOK, TOK), TOK)] = fin_r[...]
     for copy in pending:
         copy.wait_send()
 
@@ -413,14 +426,9 @@
 def per_device(
     hidden_in, cached_len, k_cache, v_cache, attn_gain, ffn_gain, wqkv, wo, wgate, wup, wdown
 ):
-    ht = hidden_in.reshape(2, TOK, 64).transpose(0, 2, 1)
-    length = cached_len[lax.axis_index("narrow")]
-    exponent = jnp.arange(HD // 2, dtype=F32) * (2.0 / HD)
-    frequency = jnp.power(10000.0, -exponent)
-    positions = (length + jnp.arange(2 * TOK, dtype=jnp.int32)).astype(F32).reshape(2, 1, TOK)
-    angles = positions * frequency[None, :, None]
-    gain1 = attn_gain.astype(F32).reshape(CHIPS, 128).T
-    gain2 = ffn_gain.astype(F32).reshape(CHIPS, 128).T
+    exponent = np.arange(HD // 2, dtype=np.float32) * np.float32(2.0 / HD)
+    frequency = np.power(np.float32(10000.0), -exponent).astype(np.float32)
+    freq = jnp.asarray(np.outer(frequency, np.arange(1, TOK + 1, dtype=np.float32)))
 
     def vm(*shape, dtype=BF16):
         return pltpu.VMEM(shape, dtype)
@@ -436,23 +444,24 @@
     out, nk, nv = pl.pallas_call(
         layer_kernel,
         out_shape=(
-            jax.ShapeDtypeStruct((2, 64, TOK), BF16),
+            jax.ShapeDtypeStruct((64, 2 * TOK), BF16),
             jax.ShapeDtypeStruct((SLOTS, HD), BF16),
             jax.ShapeDtypeStruct((SLOTS, HD), BF16),
         ),
-        in_specs=[pl.BlockSpec(memory_space=pltpu.SMEM)] + [in_vmem] * 7 + [in_hbm] * 5,
+        in_specs=[pl.BlockSpec(memory_space=pltpu.SMEM)] + [in_vmem] * 6 + [in_hbm] * 5,
         out_specs=(in_vmem, in_vmem, in_vmem),
         scratch_shapes=[
+            vm(2, 64, TOK), vm(2, 64, TOK, dtype=F32), vm(2, 64, TOK, dtype=F32),
             vm(CHIPS, 128, TOK), vm(CHIPS, 128, TOK), vm(CHIPS, 128, TOK), vm(CHIPS, 128, TOK),
             vm(NY, 2 * wqkv.shape[0], TOK), vm(2, 2 * HD, TOK), vm(2, HD, TOK),
             vm(8, SLOTS, HD), vm(8, HD, SLOTS),
             vm(8, SLOTS, TOK, dtype=F32), vm(2, TOK, TOK, dtype=F32), vm(8, TOK, dtype=F32),
             full(wqkv), full(wo), full(wgate), full(wup), full(wdown),
             vm(2, 2 * wgate.shape[0], TOK, dtype=F32),
-            vm(CHIPS, TOK, 128, dtype=F32),
-            vm(4, NY, TOK, 128), vm(3, NY, TOK, 128), vm(4, NY, TOK, 128), vm(3, NY, TOK, 128),
-            vm(3, TOK, 128), vm(3, TOK, 128), vm(128, TOK), vm(64, TOK),
-            sems(1), sems(1), sems(3, 31), sems(3, 31), sems(5), sems(5, 8), sems(5, 8),
+            vm(NZ, TOK, 512, dtype=F32),
+            vm(NZ, 3, TOK, 128), vm(NZ, 3, TOK, 128), vm(NZ - 1, TOK, 128), vm(NZ - 1, TOK, 128),
+            vm(128, TOK), vm(64, TOK),
+            sems(1), sems(1), sems(3, 32), sems(3, 32), sems(5), sems(5, 8), sems(5, 8),
             sems(2, 7), sems(2, 7), sems(4), sems(4), sems(32), sems(32),
         ],
         compiler_params=pltpu.CompilerParams(
@@ -460,11 +469,10 @@
         ),
         name="layer",
     )(
-        cached_len, ht, jnp.cos(angles), jnp.sin(angles), gain1, gain2,
+        cached_len, hidden_in.T, freq, attn_gain.reshape(CHIPS, 128), ffn_gain.reshape(CHIPS, 128),
         k_cache[0], v_cache[0], wqkv, wo, wgate, wup, wdown,
     )
-    hidden_out = out.transpose(0, 2, 1).reshape(2 * TOK, 64)
-    return (hidden_out, nk[None], nv[None])
+    return (out.T, nk[None], nv[None])
 
 
 def solution(mesh):

time: 116 us -> 102 us (0.88)
  Pallas kernels: 105 us -> 98 us
  local copies, waits for them, and re-layouts: 7.63 us -> 3.64 us
  other arithmetic: 1.63 us -> 0 us
    pallas_call x1, Pallas kernels: 105 us -> 98 us  [per_device(): pl.pallas_call(layer_kernel, out_shape=(jax.ShapeDtypeStruct((64, 2 * TOK...]
    transpose x3 -> x0, local copies, waits for them, and re-layouts: 2.07 us -> none  [the longest x1 0.73 us: per_device(): gain2 = ffn_gain.astype(F32).reshape(CHIPS, 128).T]
    reshape x1 -> x0, local copies, waits for them, and re-layouts: 1.38 us -> none  [per_device(): hidden_out = out.transpose(0, 2, 1).reshape(2 * TOK, 64)]
    unnamed x12 -> x5, local copies, waits for them, and re-layouts: 3.6 us -> 3.64 us
where the time goes in v2:
time: 102 us
  Pallas kernels  98 us (96%)
  local copies, waits for them, and re-layouts  3.64 us (4%)
    pallas_call x1, Pallas kernels, per_device(): pl.pallas_call(layer_kernel, out_shape=(jax.ShapeDtypeStruct((64, 2 * TOK...  98 us
    unnamed x5, local copies, waits for them, and re-layouts  3.64 us

profile of v2, /device:TPU:1, one launch (start us, length us, event | category | flops | bytes accessed | tf_op | source)
XLA Modules:
  0.0 102.3 jit_solution(3038936862663483093)
XLA Ops:
  0.6 98.0 %layer.1 = (bf16[64,256]{1,0:T(8,128)(2,1)}, bf16[512,128]{1,0:T(8,128)(2,1)}, bf16[512,128]{1,0:T(8,128)(2,1)}) custom-call(s32[4]{0:T(128)} %len_ref.1, bf16[64,256]{1,0:T(8,128)(2,1)} %bitcast.12, f32[64,128]{1,0:T(8,128)} %constant.2.clone.freq, bf16[32,128]{1,0:T(8,128)(2,1)} %bitcast.14, bf16[32,128]{1,0:T(8,128)(2,1)} %bitcast.15, ...), custom_call_target="tpu_custom_call" | custom-call | tf_op jit(solution)/shard_map/layer/pallas_call | solution.py:444
  98.7 1.4 %copy.18 = bf16[256,64]{0,1:T(8,128)(2,1)} copy(bf16[256,64]{0,1:T(8,128)(2,1)} %bitcast.13) | data formatting | bytes 65536
  100.0 0.0 copy-start
  100.0 1.6 %copy.19 = bf16[1,512,128]{2,1,0:T(8,128)(2,1)} copy(bf16[1,512,128]{2,1,0:T(8,128)(2,1)} %bitcast.11) | data formatting | bytes 262144
  101.6 0.0 copy-done
  101.6 0.7 copy.20
Async XLA Ops:
  100.0 1.6 %copy-start = (bf16[512,128]{1,0:T(8,128)(2,1)S(1)}, bf16[512,128]{1,0:T(8,128)(2,1)}, u32[]{:S(2)}) copy-start(bf16[512,128]{1,0:T(8,128)(2,1)} %get-tuple-element.8) | copy-start | bytes 393220

commit v3 on v2

--- a/solution.py
+++ b/solution.py
@@ -17,7 +17,6 @@
 F32 = jnp.float32
 YORDER = (0, 1, 3, 2)
 NEAR = (1, -1, 2, -2, 3, -3, 4)
-FAR = (4, 3, -3, 2, -2, 1, -1, 0)
 
 
 def dot(a, b):
@@ -30,9 +29,9 @@
 
 def layer_kernel(
     len_ref, hid, freq, gain1, gain2, kc, vc, wqkv, wo, wg, wu, wd,
-    out, nk, nv,
+    out, new_k, new_v,
     ht, cos, sin, xb, ab, hb, nb, gq, kvn, krt, ka, vt, sc, sn, ssq,
-    wqf, wof, wgf, wuf, wdf, gu, db, ys, yr, zs, zr, fin, fin_r,
+    wqf, wof, wgf, wuf, wdf, gu, db, total_f, ys, yr, zs, zr, fin, fin_r,
     p_s, p_r, ag_s, ag_r, w_l, w_s, w_r, kv_s, kv_r, q_s, q_r, rs_s, rs_r,
 ):
     wide = lax.axis_index("wide")
@@ -122,11 +121,15 @@
         arrive(f.at[xo, k, hi], w_r.at[m, 3])
         send(f.at[xo, k], f.at[xo, k], w_s.at[m, 7], w_r.at[m, 7], partner)
 
-    def w_ready(m):
-        f = full_w[m]
-        locals_w[m].wait()
-        for i, block in enumerate((x, xl, xr, xo)):
-            arrive(f.at[block, 1 - k], w_r.at[m, 4 + i])
+    blocks = (x, xl, xr, xo)
+
+    def w_ready(m, i):
+        if i == 0:
+            locals_w[m].wait()
+        arrive(full_w[m].at[blocks[i], 1 - k], w_r.at[m, 4 + i])
+
+    def rows_of(buf, i):
+        return buf[pl.ds(pl.multiple_of(8 * blocks[i], 8), 8)].reshape(1024, TOK)
 
     def all_gather(g, buf, on_chunk, extra, pumps):
         send_sem, recv_sem = ag_s.at[g], ag_r.at[g]
@@ -173,8 +176,8 @@
                     if s <= 3:
                         push_b(s, d)
                     on_chunk(c)
-            if s in pumps:
-                pumps[s]()
+                if (s, d) in pumps:
+                    pumps[s, d]()
 
     def all_gather_direct(g, buf, on_chunk, extra, pumps):
         send_sem, recv_sem = ag_s.at[g], ag_r.at[g]
@@ -262,22 +265,28 @@
         w_second(0)
         w_first(2)
 
+    def pump_second():
+        w_second(1)
+        w_first(3)
+
+    def pump_third():
+        w_third(0)
+        w_first(4)
+
     all_gather(
         0, xb, add_square(xb), before_first,
-        {3: pump_first, 5: lambda: w_third(0)},
+        {(2, 2): pump_first, (3, 2): pump_second, (5, 1): pump_third},
     )
     normalise(xb, gain1)
-    w_ready(0)
     rows_q = wqf.shape[2] * 2
     acc = jnp.zeros((rows_q, TOK), F32)
     for i in range(NX):
-        acc += dot(wqf[i].reshape(rows_q, 1024), nb[8 * i : 8 * i + 8].reshape(1024, TOK))
+        w_ready(0, i)
+        acc += dot(wqf[blocks[i]].reshape(rows_q, 1024), rows_of(nb, i))
     gq[y] = acc.astype(BF16)
 
     for d in (1, 3, 2):
         send(gq.at[y], gq.at[y], q_s.at[d - 1], q_r.at[d - 1], ypeer(d))
-    w_second(1)
-    w_first(3)
     pass_caches()
     for d in (1, 3, 2):
         arrive(gq.at[(y + NY - d) % NY], q_r.at[d - 1])
@@ -335,85 +344,81 @@
         mixed = mixed + dot(kvn[h, HD:], e.astype(BF16))
     ab[chip] = (mixed / total).astype(BF16)
 
-    def update_caches():
-        slot = lax.broadcasted_iota(jnp.int32, (SLOTS, TOK), 0) + (2 * y + k) * SLOTS
-        offset = slot - length
-        offset = jnp.where(offset < 0, offset + WINDOW, offset)
-        lane = lax.broadcasted_iota(jnp.int32, (SLOTS, TOK), 1)
-        first = jnp.where(offset == lane, 1.0, 0.0).astype(BF16)
-        second = jnp.where(offset == lane + TOK, 1.0, 0.0).astype(BF16)
-        fresh = offset < 2 * TOK
-        keys = dot_nt(first, krt[0]) + dot_nt(second, krt[1])
-        vals = dot_nt(first, kvn[0, HD:]) + dot_nt(second, kvn[1, HD:])
-        nk[...] = jnp.where(fresh, keys, kc[...].astype(F32)).astype(BF16)
-        nv[...] = jnp.where(fresh, vals, vc[...].astype(F32)).astype(BF16)
-
     def before_second():
         w_second(2)
-        w_first(4)
         w_third(1)
-        update_caches()
+        for h in range(2):
+            new_k[h] = krt[h]
+            new_v[h] = kvn[h, HD:]
 
     all_gather_direct(
         1, ab, lambda c: None, before_second,
-        {4: lambda: w_second(3), 7: lambda: w_third(2)},
+        {4: lambda: w_second(3)},
     )
-    w_ready(1)
     rows_o = wof.shape[2] * 2
     acc = xb[chip].astype(F32)
     proj = jnp.zeros((rows_o, TOK), F32)
     for i in range(NX):
-        proj += dot(wof[i].reshape(rows_o, 1024), ab[8 * i : 8 * i + 8].reshape(1024, TOK))
+        w_ready(1, i)
+        proj += dot(wof[blocks[i]].reshape(rows_o, 1024), rows_of(ab, i))
     hb[chip] = (acc + proj).astype(BF16)
     ssq[...] = jnp.zeros_like(ssq)
 
     all_gather_direct(
         2, hb, add_square(hb), lambda: None,
-        {3: lambda: w_second(4), 7: lambda: w_third(3)},
+        {0: lambda: w_second(4), 4: lambda: w_third(2), 7: lambda: w_third(3)},
     )
     normalise(hb, gain2)
-    w_ready(2)
-    w_ready(3)
     rows_f = wgf.shape[2] * 2
-    gu[...] = jnp.zeros_like(gu)
-
-    def hidden_step(i, carry):
-        block = nb[pl.ds(pl.multiple_of(8 * i, 8), 8)].reshape(1024, TOK)
-        gu[0] += dot(wgf[i].reshape(rows_f, 1024), block)
-        gu[1] += dot(wuf[i].reshape(rows_f, 1024), block)
-        return carry
-
-    lax.fori_loop(0, NX, hidden_step, 0)
+    for i in range(NX):
+        block = rows_of(nb, i)
+        for m, f in ((2, wgf), (3, wuf)):
+            w_ready(m, i)
+            part = dot(f[blocks[i]].reshape(rows_f, 1024), block)
+            gu[m - 2] = part if i == 0 else gu[m - 2] + part
     gate = gu[0]
     act = (gate / (1.0 + jnp.exp(-gate))) * gu[1]
     act_t = jnp.transpose(act).astype(BF16)
-    w_third(4)
-    w_ready(4)
-
-    for i, r in enumerate(FAR):
-        zz = (z + r + NZ) % NZ
-        cols = pl.ds(pl.multiple_of((zz % 2) * 512, 512), 512)
-        db[i] = dot(act_t, wdf[zz // 2, :, :, cols].reshape(rows_f, 512))
+
+    for i in range(NZ):
+        block = blocks[i // 2]
+        if i == 4:
+            w_third(4)
+        if i % 2 == 0:
+            w_ready(4, i // 2)
+        cols = pl.ds((i % 2) * 512, 512)
+        db[i] = dot(act_t, wdf[block, :, :, cols].reshape(rows_f, 512))
         for d in (2, 1, 3):
             col = pl.ds(pl.multiple_of(((y + d) % NY) * 128, 128), 128)
             ys[i, d - 1] = db[i, :, col].astype(BF16)
             n = 3 * i + d - 1
             send(ys.at[i, d - 1], yr.at[i, d - 1], rs_s.at[n], rs_r.at[n], ypeer(d))
     own_col = pl.ds(pl.multiple_of(y * 128, 128), 128)
-    whole = None
-    for i, r in enumerate(FAR):
+    for i in range(NZ):
+        zz = 2 * blocks[i // 2] + i % 2
+        disp = (zz - z + NZ) % NZ
         v = db[i, :, own_col]
         for d in (1, 3, 2):
             arrive(yr.at[i, d - 1], rs_r.at[3 * i + d - 1])
             v = v + yr[i, d - 1].astype(F32)
-        if r == 0:
-            whole = v
-        else:
-            zs[i] = v.astype(BF16)
-            send(zs.at[i], zr.at[i], rs_s.at[24 + i], rs_r.at[24 + i], zpeer(r))
-    for i in reversed(range(NZ - 1)):
-        arrive(zr.at[i], rs_r.at[24 + i])
-        whole = whole + zr[i].astype(F32)
+        zs[disp] = v.astype(BF16)
+
+        @pl.when(disp == 0)
+        def _():
+            total_f[...] = v
+
+        @pl.when(disp != 0)
+        def _():
+            pltpu.make_async_remote_copy(
+                src_ref=zs.at[disp], dst_ref=zr.at[disp],
+                send_sem=rs_s.at[23 + disp], recv_sem=rs_r.at[23 + disp],
+                device_id=dev(zz, y, k, x), device_id_type=pl.DeviceIdType.MESH,
+            ).start()
+
+    whole = total_f[...]
+    for dz in NEAR:
+        arrive(zr.at[dz % NZ], rs_r.at[23 + dz % NZ])
+        whole = whole + zr[dz % NZ].astype(F32)
     fin[...] = (hb[chip].astype(F32) + jnp.transpose(whole)).astype(BF16)
     send(fin.at[other_rows], fin_r, rs_s.at[31], rs_r.at[31], partner)
     out[:, pl.ds(pl.multiple_of(k * TOK, TOK), TOK)] = fin[half_rows, :]
@@ -421,6 +426,27 @@
     out[:, pl.ds(pl.multiple_of((1 - k) * TOK, TOK), TOK)] = fin_r[...]
     for copy in pending:
         copy.wait_send()
+    for i in range(1, NZ):
+        pltpu.make_async_remote_copy(
+            src_ref=zs.at[i], dst_ref=zr.at[i], send_sem=rs_s.at[23 + i], recv_sem=rs_r.at[23 + i],
+            device_id=partner, device_id_type=pl.DeviceIdType.MESH,
+        ).wait_send()
+
+
+def cache_kernel(len_ref, hid, new_k, new_v, kc, vc, out, nk, nv):
+    length = len_ref[lax.axis_index("narrow")]
+    slot = lax.broadcasted_iota(jnp.int32, (SLOTS, TOK), 0) + lax.axis_index("wide") % 8 * SLOTS
+    offset = slot - length
+    offset = jnp.where(offset < 0, offset + WINDOW, offset)
+    lane = lax.broadcasted_iota(jnp.int32, (SLOTS, TOK), 1)
+    first = jnp.where(offset == lane, 1.0, 0.0).astype(BF16)
+    second = jnp.where(offset == lane + TOK, 1.0, 0.0).astype(BF16)
+    fresh = offset < 2 * TOK
+    keys = dot_nt(first, new_k[0]) + dot_nt(second, new_k[1])
+    vals = dot_nt(first, new_v[0]) + dot_nt(second, new_v[1])
+    nk[...] = jnp.where(fresh, keys, kc[...].astype(F32)).astype(BF16)
+    nv[...] = jnp.where(fresh, vals, vc[...].astype(F32)).astype(BF16)
+    out[...] = hid[...]
 
 
 def per_device(
@@ -441,12 +467,12 @@
 
     in_vmem = pl.BlockSpec(memory_space=pltpu.VMEM)
     in_hbm = pl.BlockSpec(memory_space=pl.ANY)
-    out, nk, nv = pl.pallas_call(
+    out, new_k, new_v = pl.pallas_call(
         layer_kernel,
         out_shape=(
             jax.ShapeDtypeStruct((64, 2 * TOK), BF16),
-            jax.ShapeDtypeStruct((SLOTS, HD), BF16),
-            jax.ShapeDtypeStruct((SLOTS, HD), BF16),
+            jax.ShapeDtypeStruct((2, HD, TOK), BF16),
+            jax.ShapeDtypeStruct((2, HD, TOK), BF16),
         ),
         in_specs=[pl.BlockSpec(memory_space=pltpu.SMEM)] + [in_vmem] * 6 + [in_hbm] * 5,
         out_specs=(in_vmem, in_vmem, in_vmem),
@@ -458,8 +484,8 @@
             vm(8, SLOTS, TOK, dtype=F32), vm(2, TOK, TOK, dtype=F32), vm(8, TOK, dtype=F32),
             full(wqkv), full(wo), full(wgate), full(wup), full(wdown),
             vm(2, 2 * wgate.shape[0], TOK, dtype=F32),
-            vm(NZ, TOK, 512, dtype=F32),
-            vm(NZ, 3, TOK, 128), vm(NZ, 3, TOK, 128), vm(NZ - 1, TOK, 128), vm(NZ - 1, TOK, 128),
+            vm(NZ, TOK, 512, dtype=F32), vm(TOK, 128, dtype=F32),
+            vm(NZ, 3, TOK, 128), vm(NZ, 3, TOK, 128), vm(NZ, TOK, 128), vm(NZ, TOK, 128),
             vm(128, TOK), vm(64, TOK),
             sems(1), sems(1), sems(3, 32), sems(3, 32), sems(5), sems(5, 8), sems(5, 8),
             sems(2, 7), sems(2, 7), sems(4), sems(4), sems(32), sems(32),
@@ -472,6 +498,17 @@
         cached_len, hidden_in.T, freq, attn_gain.reshape(CHIPS, 128), ffn_gain.reshape(CHIPS, 128),
         k_cache[0], v_cache[0], wqkv, wo, wgate, wup, wdown,
     )
+    out, nk, nv = pl.pallas_call(
+        cache_kernel,
+        out_shape=(
+            jax.ShapeDtypeStruct((64, 2 * TOK), BF16),
+            jax.ShapeDtypeStruct((SLOTS, HD), BF16),
+            jax.ShapeDtypeStruct((SLOTS, HD), BF16),
+        ),
+        in_specs=[pl.BlockSpec(memory_space=pltpu.SMEM)] + [in_vmem] * 5,
+        out_specs=(in_vmem, in_vmem, in_vmem),
+        name="caches",
+    )(cached_len, out, new_k, new_v, k_cache[0], v_cache[0])
     return (out.T, nk[None], nv[None])
 
 

time: 102 us -> 96.1 us (0.942)
  the two profiles are of different devices: /device:TPU:1 before, /device:TPU:5 now
where the time goes in v3:
time: 96.1 us; the launch traced here: 95.9 us
  Pallas kernels  95.3 us (99%)
    pallas_call x1, Pallas kernels, per_device(): pl.pallas_call(layer_kernel, out_shape=(jax.ShapeDtypeStruct((64, 2 * TOK...  93.2 us
    pallas_call x1, Pallas kernels, per_device(): pl.pallas_call(cache_kernel, out_shape=(jax.ShapeDtypeStruct((64, 2 * TOK...  2.07 us

profile of v3, /device:TPU:5, one launch (start us, length us, event | category | flops | bytes accessed | tf_op | source)
XLA Modules:
  0.0 95.9 jit_solution(11476767583652452974)
XLA Ops:
  0.6 93.2 %layer.1 = (bf16[64,256]{1,0:T(8,128)(2,1)}, bf16[2,128,128]{2,1,0:T(8,128)(2,1)}, bf16[2,128,128]{2,1,0:T(8,128)(2,1)}) custom-call(s32[4]{0:T(128)} %len_ref.3, bf16[64,256]{1,0:T(8,128)(2,1)} %bitcast.12, f32[64,128]{1,0:T(8,128)} %constant.2.clone.freq, bf16[32,128]{1,0:T(8,128)(2,1)} %bitcast.13, bf16[32,128]{1,0:T(8,128)(2,1)} %bitcast.14, ...), custom_call_target="tpu_custom_call" | custom-call | tf_op jit(solution)/shard_map/layer/pallas_call | solution.py:470
  93.9 2.1 %caches.1 = (bf16[64,256]{1,0:T(8,128)(2,1)}, bf16[512,128]{1,0:T(8,128)(2,1)}, bf16[512,128]{1,0:T(8,128)(2,1)}) custom-call(s32[4]{0:T(128)} %len_ref.3, bf16[64,256]{1,0:T(8,128)(2,1)} %get-tuple-element.9.hid, bf16[2,128,128]{2,1,0:T(8,128)(2,1)} %get-tuple-element.10.new_k, bf16[2,128,128]{2,1,0:T(8,128)(2,1)} %get-tuple-element.11.new_v, ...), custom_call_target="tpu_custom_call" | custom-call | tf_op jit(solution)/shard_map/caches/pallas_call | solution.py:501

commit v4 on v3

--- a/solution.py
+++ b/solution.py
@@ -16,6 +16,7 @@
 BF16 = jnp.bfloat16
 F32 = jnp.float32
 YORDER = (0, 1, 3, 2)
+UP_FROM = 3
 NEAR = (1, -1, 2, -2, 3, -3, 4)
 
 
@@ -28,10 +29,10 @@
 
 
 def layer_kernel(
-    len_ref, hid, freq, gain1, gain2, kc, vc, wqkv, wo, wg, wu, wd,
+    len_ref, hid, freq_h, gain1_h, gain2_h, kc, vc, wqkv, wo, wg, wu, wd,
     out, new_k, new_v,
-    ht, cos, sin, xb, ab, hb, nb, gq, kvn, krt, ka, vt, sc, sn, ssq,
-    wqf, wof, wgf, wuf, wdf, gu, db, total_f, ys, yr, zs, zr, fin, fin_r,
+    freq, gain1, gain2, vl, l_sem, ht, cos, sin, xb, ab, hb, nb, gq, kvn, krt, ka, vt, sc, sn, ssq,
+    wqf, wof, wgf, wuf, wdf, gb, pj, gu, db, total_f, ys, yr, zs, zr, fin, fin_r,
     p_s, p_r, ag_s, ag_r, w_l, w_s, w_r, kv_s, kv_r, q_s, q_r, rs_s, rs_r,
 ):
     wide = lax.axis_index("wide")
@@ -63,14 +64,20 @@
     dev_xl = dev(z, y, k, xl)
 
     pending = []
-
-    def send(src, dst, s_sem, r_sem, device):
+    pending_w = {m: [] for m in range(5)}
+
+    def drain(copies):
+        for copy in copies:
+            copy.wait_send()
+        copies.clear()
+
+    def send(src, dst, s_sem, r_sem, device, started=pending):
         copy = pltpu.make_async_remote_copy(
             src_ref=src, dst_ref=dst, send_sem=s_sem, recv_sem=r_sem,
             device_id=device, device_id_type=pl.DeviceIdType.MESH,
         )
         copy.start()
-        pending.append(copy)
+        started.append(copy)
 
     def arrive(dst, r_sem):
         pltpu.make_async_remote_copy(
@@ -82,10 +89,15 @@
     greet = [partner, ypeer(1), ypeer(2), ypeer(3), dev_xr, dev_xl] + [zpeer(d) for d in NEAR]
     for peer in greet:
         pl.semaphore_signal(barrier, inc=1, device_id=peer, device_id_type=pl.DeviceIdType.MESH)
-    for h in range(2):
-        ht[h] = hid[:, h * TOK : (h + 1) * TOK]
-    vt[2 * y + k] = jnp.transpose(vc[...].astype(F32)).astype(BF16)
-    ka[2 * y + k] = kc[...]
+    inward = [
+        pltpu.make_async_copy(src, dst, l_sem.at[i])
+        for i, (src, dst) in enumerate((
+            (hid.at[:, pl.ds(0, TOK)], ht.at[0]), (hid.at[:, pl.ds(TOK, TOK)], ht.at[1]),
+            (kc, ka.at[2 * y + k]), (vc, vl), (freq_h, freq), (gain1_h, gain1), (gain2_h, gain2),
+        ))
+    ]
+    for copy in inward:
+        copy.start()
     ssq[...] = jnp.zeros_like(ssq)
     pl.semaphore_wait(barrier, len(greet))
 
@@ -98,20 +110,20 @@
         copy = pltpu.make_async_copy(o, f.at[x, k], w_l.at[m])
         copy.start()
         locals_w.append(copy)
-        send(o, f.at[x, k], w_s.at[m, 0], w_r.at[m, 0], dev_xr)
-        send(o, f.at[x, k], w_s.at[m, 1], w_r.at[m, 1], dev_xl)
-        send(o, f.at[x, k], w_s.at[m, 4], w_r.at[m, 4], partner)
+        send(o, f.at[x, k], w_s.at[m, 0], w_r.at[m, 0], dev_xr, pending_w[m])
+        send(o, f.at[x, k], w_s.at[m, 1], w_r.at[m, 1], dev_xl, pending_w[m])
+        send(o, f.at[x, k], w_s.at[m, 4], w_r.at[m, 4], partner, pending_w[m])
 
     def w_second(m):
         f = full_w[m]
         half = f.shape[2] // 2
         lo, hi = pl.ds(0, half), pl.ds(half, half)
         arrive(f.at[xl, k], w_r.at[m, 0])
-        send(f.at[xl, k, lo], f.at[xl, k, lo], w_s.at[m, 2], w_r.at[m, 2], dev_xr)
-        send(f.at[xl, k], f.at[xl, k], w_s.at[m, 5], w_r.at[m, 5], partner)
+        send(f.at[xl, k, lo], f.at[xl, k, lo], w_s.at[m, 2], w_r.at[m, 2], dev_xr, pending_w[m])
+        send(f.at[xl, k], f.at[xl, k], w_s.at[m, 5], w_r.at[m, 5], partner, pending_w[m])
         arrive(f.at[xr, k], w_r.at[m, 1])
-        send(f.at[xr, k, hi], f.at[xr, k, hi], w_s.at[m, 3], w_r.at[m, 3], dev_xl)
-        send(f.at[xr, k], f.at[xr, k], w_s.at[m, 6], w_r.at[m, 6], partner)
+        send(f.at[xr, k, hi], f.at[xr, k, hi], w_s.at[m, 3], w_r.at[m, 3], dev_xl, pending_w[m])
+        send(f.at[xr, k], f.at[xr, k], w_s.at[m, 6], w_r.at[m, 6], partner, pending_w[m])
 
     def w_third(m):
         f = full_w[m]
@@ -119,7 +131,7 @@
         lo, hi = pl.ds(0, half), pl.ds(half, half)
         arrive(f.at[xo, k, lo], w_r.at[m, 2])
         arrive(f.at[xo, k, hi], w_r.at[m, 3])
-        send(f.at[xo, k], f.at[xo, k], w_s.at[m, 7], w_r.at[m, 7], partner)
+        send(f.at[xo, k], f.at[xo, k], w_s.at[m, 7], w_r.at[m, 7], partner, pending_w[m])
 
     blocks = (x, xl, xr, xo)
 
@@ -179,7 +191,7 @@
                 if (s, d) in pumps:
                     pumps[s, d]()
 
-    def all_gather_direct(g, buf, on_chunk, extra, pumps):
+    def all_gather_direct(g, buf, on_chunk, extra, pumps, on_plane):
         send_sem, recv_sem = ag_s.at[g], ag_r.at[g]
 
         def row(dz, dy):
@@ -209,6 +221,7 @@
                 on_chunk(row(-dz, -d))
             if i in pumps:
                 pumps[i]()
+            on_plane(i, (z - dz + NZ) % NZ)
 
     def add_square(buf):
         def run(c):
@@ -226,6 +239,8 @@
 
     half_rows = pl.ds(pl.multiple_of(k * 64, 64), 64)
     other_rows = pl.ds(pl.multiple_of((1 - k) * 64, 64), 64)
+    inward[0].wait()
+    inward[1].wait()
     send(ht.at[1 - k], xb.at[chip, half_rows], p_s.at[0], p_r.at[0], partner)
     xb[chip, half_rows, :] = ht[k]
     w_first(0)
@@ -254,6 +269,9 @@
                 arrive(buf.at[p], kv_r.at[i, 3 + d])
 
     def before_first():
+        for copy in inward[2:]:
+            copy.wait()
+        vt[2 * y + k] = jnp.transpose(vl[...].astype(F32)).astype(BF16)
         send_caches()
         for h in range(2):
             t = lax.broadcasted_iota(jnp.int32, (1, TOK), 1) + (TOK * h + len_ref[x])
@@ -271,7 +289,6 @@
 
     def pump_third():
         w_third(0)
-        w_first(4)
 
     all_gather(
         0, xb, add_square(xb), before_first,
@@ -344,41 +361,90 @@
         mixed = mixed + dot(kvn[h, HD:], e.astype(BF16))
     ab[chip] = (mixed / total).astype(BF16)
 
+    count_first = len(pending)
+    rows_o = wof.shape[2] * 2
+    rows_f = wgf.shape[2] * 2
+
+    def plane_of(f, rows, zz):
+        cols = pl.ds(pl.multiple_of((zz % 2) * 512, 512), 512)
+        return f[zz // 2, :, :, cols].reshape(rows, 512)
+
+    def plane_rows(buf, zz):
+        return buf[pl.ds(pl.multiple_of(NY * zz, NY), NY)].reshape(NY * 128, TOK)
+
+    def project(i, zz):
+        if i == 0:
+            for j in range(NX):
+                w_ready(1, j)
+        part = dot(plane_of(wof, rows_o, zz), plane_rows(ab, zz))
+        pj[...] = part if i == 0 else pj[...] + part
+
+    def up_then_down():
+        w_second(3)
+        w_first(4)
+
     def before_second():
         w_second(2)
         w_third(1)
+        drain(pending[:count_first])
+        del pending[:count_first]
+        gains = jnp.transpose(gain2[...].astype(F32))
+        for c in range(CHIPS):
+            gb[c] = jnp.broadcast_to(gains[:, c : c + 1], (128, TOK))
         for h in range(2):
             new_k[h] = krt[h]
             new_v[h] = kvn[h, HD:]
 
     all_gather_direct(
         1, ab, lambda c: None, before_second,
-        {4: lambda: w_second(3)},
+        {4: up_then_down, 7: lambda: w_third(2)}, project,
     )
-    rows_o = wof.shape[2] * 2
-    acc = xb[chip].astype(F32)
-    proj = jnp.zeros((rows_o, TOK), F32)
-    for i in range(NX):
-        w_ready(1, i)
-        proj += dot(wof[blocks[i]].reshape(rows_o, 1024), rows_of(ab, i))
-    hb[chip] = (acc + proj).astype(BF16)
+    hb[chip] = (xb[chip].astype(F32) + pj[...]).astype(BF16)
     ssq[...] = jnp.zeros_like(ssq)
 
+    count_second = len(pending)
+
+    def before_third():
+        drain(pending[:count_second])
+        del pending[:count_second]
+        drain(pending_w[0])
+        drain(pending_w[1])
+
+    def square_and_gain(c):
+        v = hb[c].astype(F32)
+        ssq[...] += jnp.sum((v * v).reshape(16, 8, TOK), axis=0)
+        nb[c] = (v * gb[c]).astype(BF16)
+
+    def hidden_part(m, f, i, zz):
+        part = dot(plane_of(f, rows_f, zz), plane_rows(nb, zz))
+        gu[m] = part if i == 0 else gu[m] + part
+
+    planes = []
+
+    def hidden_plane(i, zz):
+        planes.append(zz)
+        if i == 0:
+            for j in range(NX):
+                w_ready(2, j)
+        hidden_part(0, wgf, i, zz)
+        if i == UP_FROM:
+            for j in range(NX):
+                w_ready(3, j)
+            for n in range(i):
+                hidden_part(1, wuf, n, planes[n])
+        if i >= UP_FROM:
+            hidden_part(1, wuf, i, zz)
+
     all_gather_direct(
-        2, hb, add_square(hb), lambda: None,
-        {0: lambda: w_second(4), 4: lambda: w_third(2), 7: lambda: w_third(3)},
+        2, hb, square_and_gain, before_third,
+        {0: lambda: w_third(3), 6: lambda: w_second(4)}, hidden_plane,
     )
-    normalise(hb, gain2)
-    rows_f = wgf.shape[2] * 2
-    for i in range(NX):
-        block = rows_of(nb, i)
-        for m, f in ((2, wgf), (3, wuf)):
-            w_ready(m, i)
-            part = dot(f[blocks[i]].reshape(rows_f, 1024), block)
-            gu[m - 2] = part if i == 0 else gu[m - 2] + part
-    gate = gu[0]
-    act = (gate / (1.0 + jnp.exp(-gate))) * gu[1]
+    r = lax.rsqrt(jnp.sum(ssq[...], axis=0, keepdims=True) * (1.0 / (CHIPS * 128)) + 1e-05)
+    gate = gu[0] * r
+    act = (gate / (1.0 + jnp.exp(-gate))) * (gu[1] * r)
     act_t = jnp.transpose(act).astype(BF16)
+
+    count_third = len(pending)
 
     for i in range(NZ):
         block = blocks[i // 2]
@@ -394,6 +460,10 @@
             n = 3 * i + d - 1
             send(ys.at[i, d - 1], yr.at[i, d - 1], rs_s.at[n], rs_r.at[n], ypeer(d))
     own_col = pl.ds(pl.multiple_of(y * 128, 128), 128)
+    drain(pending[:count_third])
+    del pending[:count_third]
+    drain(pending_w[2])
+    drain(pending_w[3])
     for i in range(NZ):
         zz = 2 * blocks[i // 2] + i % 2
         disp = (zz - z + NZ) % NZ
@@ -424,8 +494,8 @@
     out[:, pl.ds(pl.multiple_of(k * TOK, TOK), TOK)] = fin[half_rows, :]
     arrive(fin_r, rs_r.at[31])
     out[:, pl.ds(pl.multiple_of((1 - k) * TOK, TOK), TOK)] = fin_r[...]
-    for copy in pending:
-        copy.wait_send()
+    drain(pending)
+    drain(pending_w[4])
     for i in range(1, NZ):
         pltpu.make_async_remote_copy(
             src_ref=zs.at[i], dst_ref=zr.at[i], send_sem=rs_s.at[23 + i], recv_sem=rs_r.at[23 + i],
@@ -474,15 +544,17 @@
             jax.ShapeDtypeStruct((2, HD, TOK), BF16),
             jax.ShapeDtypeStruct((2, HD, TOK), BF16),
         ),
-        in_specs=[pl.BlockSpec(memory_space=pltpu.SMEM)] + [in_vmem] * 6 + [in_hbm] * 5,
+        in_specs=[pl.BlockSpec(memory_space=pltpu.SMEM)] + [in_hbm] * 11,
         out_specs=(in_vmem, in_vmem, in_vmem),
         scratch_shapes=[
+            vm(HD // 2, TOK, dtype=F32), vm(CHIPS, 128), vm(CHIPS, 128), vm(SLOTS, HD), sems(7),
             vm(2, 64, TOK), vm(2, 64, TOK, dtype=F32), vm(2, 64, TOK, dtype=F32),
             vm(CHIPS, 128, TOK), vm(CHIPS, 128, TOK), vm(CHIPS, 128, TOK), vm(CHIPS, 128, TOK),
             vm(NY, 2 * wqkv.shape[0], TOK), vm(2, 2 * HD, TOK), vm(2, HD, TOK),
             vm(8, SLOTS, HD), vm(8, HD, SLOTS),
             vm(8, SLOTS, TOK, dtype=F32), vm(2, TOK, TOK, dtype=F32), vm(8, TOK, dtype=F32),
             full(wqkv), full(wo), full(wgate), full(wup), full(wdown),
+            vm(CHIPS, 128, TOK, dtype=F32), vm(128, TOK, dtype=F32),
             vm(2, 2 * wgate.shape[0], TOK, dtype=F32),
             vm(NZ, TOK, 512, dtype=F32), vm(TOK, 128, dtype=F32),
             vm(NZ, 3, TOK, 128), vm(NZ, 3, TOK, 128), vm(NZ, TOK, 128), vm(NZ, TOK, 128),

time: 96.1 us -> 92.2 us (0.959)
  Pallas kernels: 95.3 us -> 91.5 us
    pallas_call x1, Pallas kernels: 93.2 us -> 89.4 us  [per_device(): pl.pallas_call(layer_kernel, out_shape=(jax.ShapeDtypeStruct((64, 2 * TOK...]
where the time goes in v4:
time: 92.2 us; the launch traced here: 92.1 us
  Pallas kernels  91.5 us (99%)
    pallas_call x1, Pallas kernels, per_device(): pl.pallas_call(layer_kernel, out_shape=(jax.ShapeDtypeStruct((64, 2 * TOK...  89.4 us
    pallas_call x1, Pallas kernels, per_device(): pl.pallas_call(cache_kernel, out_shape=(jax.ShapeDtypeStruct((64, 2 * TOK...  2.07 us

profile of v4, /device:TPU:5, one launch (start us, length us, event | category | flops | bytes accessed | tf_op | source)
XLA Modules:
  0.0 92.1 jit_solution(11799744902694887016)
XLA Ops:
  0.6 89.4 %layer.1 = (bf16[64,256]{1,0:T(8,128)(2,1)}, bf16[2,128,128]{2,1,0:T(8,128)(2,1)}, bf16[2,128,128]{2,1,0:T(8,128)(2,1)}) custom-call(s32[4]{0:T(128)} %len_ref.3, bf16[64,256]{1,0:T(8,128)(2,1)} %bitcast.12, f32[64,128]{1,0:T(8,128)} %constant.2.clone.freq_h, bf16[32,128]{1,0:T(8,128)(2,1)} %bitcast.13, bf16[32,128]{1,0:T(8,128)(2,1)} %bitcast.14, ...), custom_call_target="tpu_custom_call" | custom-call | tf_op jit(solution)/shard_map/layer/pallas_call | solution.py:540
  90.1 2.1 %caches.1 = (bf16[64,256]{1,0:T(8,128)(2,1)}, bf16[512,128]{1,0:T(8,128)(2,1)}, bf16[512,128]{1,0:T(8,128)(2,1)}) custom-call(s32[4]{0:T(128)} %len_ref.3, bf16[64,256]{1,0:T(8,128)(2,1)} %get-tuple-element.9.hid, bf16[2,128,128]{2,1,0:T(8,128)(2,1)} %get-tuple-element.10.new_k, bf16[2,128,128]{2,1,0:T(8,128)(2,1)} %get-tuple-element.11.new_v, ...), custom_call_target="tpu_custom_call" | custom-call | tf_op jit(solution)/shard_map/caches/pallas_call | solution.py:573
